TPU v7x, 32 devices: a whole 2x2x4 slice. The times are simulated.
32 devices in a mesh: member: 2 (over x), slab: 16 (over z, y, core).
Axes of the slice: x: 2, y: 2, z: 4, core: 2. Of those that a mesh axis runs over, the one named last changes fastest.
Arguments:
- prior_ensemble_fields: float32 [64, 6, 128, 1, 1024], P('member', None, 'slab'), may hold values from -6 to 6
- params: float32 [64, 12], P('member'), may hold values from -3 to 3
- influence: int32 [12, 6], replicated, may hold values 0 or 1
- obs_cell: int32 [128, 2, 128], P('slab', 'member'), may hold values from 0 to 3071
- obs_value: float32 [128, 2, 128], P('slab', 'member'), may hold values from -6 to 6
- obs_prec: float32 [128, 2, 128], P('slab', 'member'), may hold values from 0.5 to 4
- cutoff: int32 [128], P('slab'), may hold values from 4 to 8, as said below
Outputs:
- analysis: bfloat16 [64, 6, 128, 1, 1024], P('member', None, 'slab')
- param_analysis: float32 [64, 12], P('member')
Inputs may be any that keep to these rules, and one draw needn't show every extreme that they name: `obs_cell`: index = field * 512 + level * 512 + column within the block. `cutoff`: 8 is reached by some rows.
All inputs are finite; a program needn't handle non-finite values.
Results may differ from a plain program's by a relative error of at most 0.0056.
Values may be sent and summed in bfloat16 or wider, within the bound.
No kernel may reach another device: no remote copies, remote signals or barrier semaphores. Data moves between devices by JAX's collectives and lax.ppermute only.
A program may use at most 128 MiB of HBM per device.

v0:
```python
import math

import jax
import jax.numpy as jnp
from jax import lax
from jax.sharding import PartitionSpec as P

HALO = 8
STEPS = 4
NS_STEPS = 5


diffusion = 0.2
advection = 0.15
vertical = 0.1
coupling = 0.2


def with_halo(block, sides, width):
    for axis, dim in sides:
        count = lax.axis_size(axis)
        forward = [(i, i + 1) for i in range(count - 1)]
        backward = [(target, source) for source, target in forward]
        low = lax.ppermute(
            lax.slice_in_dim(block, block.shape[dim] - width, None, axis=dim), axis, forward
        )
        high = lax.ppermute(lax.slice_in_dim(block, 0, width, axis=dim), axis, backward)
        block = jnp.concatenate([low, block, high], axis=dim)
    return block


def advance(current, dynamics_parameter):
    middle = current[:, :, 1:-1]
    upper = current[:, :, 2:]
    lower = current[:, :, :-2]
    right_col = jnp.roll(middle, -1, 4)
    left_col = jnp.roll(middle, 1, 4)
    laplace = upper + lower + right_col + left_col - 4.0 * middle
    return (
        middle
        + diffusion * laplace
        - advection * (right_col - left_col)
        + vertical * (jnp.roll(middle, 1, 3) - middle)
        + coupling * dynamics_parameter[:, :, None, None, None] * jnp.roll(middle, -1, 1)
    )


def body(prior_ensemble_fields, params, influence, obs_cell, obs_value, obs_prec, cutoff):
    highest = lax.Precision.HIGHEST
    members_here = prior_ensemble_fields.shape[0]
    rows = prior_ensemble_fields.shape[2]
    dynamics_parameter = jnp.dot(params, influence.astype(jnp.float32), precision=highest)
    prognostic_vector = prior_ensemble_fields
    for step_idx in range(STEPS):
        padded = with_halo(prognostic_vector, (("slab", 2),), 1)
        prognostic_vector = advance(padded, dynamics_parameter)
    propagate_timestep = prognostic_vector.astype(jnp.bfloat16)
    latitude_band = lax.all_to_all(
        propagate_timestep, "member", split_axis=4, concat_axis=0, tiled=True
    )
    xfull = latitude_band.astype(jnp.float32)
    ensemble = xfull.shape[0]
    block_cols = xfull.shape[4]
    levels_here = xfull.shape[3]
    xbar = jnp.mean(xfull, axis=0)
    xpert = xfull - xbar
    cells = obs_cell[:, 0, :]
    values = obs_value[:, 0, :]
    precs = obs_prec[:, 0, :]
    kinds = cells // (levels_here * block_cols)
    levels = cells // block_cols % levels_here
    columns = cells % block_cols
    row_index = jnp.arange(rows, dtype=jnp.int32)[:, None]
    ens_obs = xfull[:, kinds, row_index, levels, columns]
    ybar = jnp.mean(ens_obs, axis=0)
    ypert = ens_obs - ybar
    weighted = precs * (values - ybar)
    radius = cutoff.astype(jnp.float32)
    gram = jnp.einsum("ero,fro->ref", ypert * precs[None], ypert, precision=highest)
    gvec = jnp.einsum("ero,ro->re", ypert, weighted, precision=highest)
    stacked = jnp.concatenate([gram, gvec[:, None, :]], 1)
    wide = with_halo(stacked, (("slab", 0),), HALO)
    local = jnp.zeros_like(stacked)
    for offset in range(-HALO, HALO + 1):
        weight = jnp.maximum(0.0, 1.0 - abs(offset) / (radius + 1.0))
        local = local + weight[:, None, None] * wide[HALO + offset : HALO + offset + rows]
    gram_loc = local[:, :ensemble]
    gvec_loc = local[:, ensemble]
    eye_mat = jnp.eye(ensemble, dtype=jnp.float32)
    amat = (ensemble - 1.0) * eye_mat + gram_loc
    scale = jnp.sqrt(jnp.sum(amat * amat, axis=(1, 2)))
    ymat = amat / scale[:, None, None]
    zmat = jnp.broadcast_to(eye_mat, amat.shape)
    for step_idx in range(NS_STEPS):
        middle = 1.5 * eye_mat - 0.5 * jnp.matmul(zmat, ymat, precision=highest)
        ymat = jnp.matmul(ymat, middle, precision=highest)
        zmat = jnp.matmul(middle, zmat, precision=highest)
    wpert = math.sqrt(ensemble - 1.0) * zmat / jnp.sqrt(scale)[:, None, None]
    inner = jnp.matmul(zmat, gvec_loc[:, :, None], precision=highest)
    wbar = jnp.matmul(zmat, inner, precision=highest)[:, :, 0] / scale[:, None]
    weights = wpert + wbar[:, :, None]
    update = jnp.einsum("jfrlc,rje->efrlc", xpert, weights, precision=highest)
    analysed = (xbar + update).astype(jnp.bfloat16)
    analysis = lax.all_to_all(analysed, "member", split_axis=0, concat_axis=4, tiled=True)
    every_param = lax.all_gather(params, "member", axis=0, tiled=True)
    pbar = jnp.mean(every_param, axis=0)
    ppert = every_param - pbar
    weight_rows = jnp.sum(weights, axis=0)
    regions = rows * lax.axis_size("slab") * lax.axis_size("member")
    start = lax.axis_index("member") * members_here
    summed = lax.psum(weight_rows, ("member", "slab")) / regions
    own_cols = lax.dynamic_slice_in_dim(summed, start, members_here, 1)
    param_analysis = pbar + jnp.einsum("jk,je->ek", ppert, own_cols, precision=highest)
    return (analysis, param_analysis)


def solution(mesh):
    in_specs = (
        P("member", None, "slab", None, None),
        P("member", None),
        P(),
        P("slab", "member", None),
        P("slab", "member", None),
        P("slab", "member", None),
        P("slab"),
    )
    out_specs = (P("member", None, "slab", None, None), P("member", None))
    return jax.shard_map(body, mesh=mesh, in_specs=in_specs, out_specs=out_specs, check_vma=False)
```

profile of v0, /device:TPU:0, one launch (start us, length us, event | category | flops | bytes accessed | tf_op | source)
XLA Modules:
  0.0 462.0 jit_solution(5289665524190053646)
XLA Ops:
  0.6 6.5 %copy.281 = f32[32,6,8,1,1024]{4,0,3,2,1:T(8,128)S(1)} copy(f32[32,6,8,1,1024]{4,3,2,1,0:T(1,128)} %param.7) | data formatting | bytes 12582912 | tf_op args[0]
  7.2 2.7 copy-done.3
  12.4 4.0 collective-permute-start.1
  16.4 18.9 %fusion.108 = (f32[32,6,8,1,1023]{4,3,2,1,0:T(1,128)}, f32[32,6,8,1,1023]{4,3,2,1,0:T(1,128)}) fusion(f32[32,6,8,1,1024]{4,3,2,1,0:T(1,128)S(1)} %copy-done.2), kind=kLoop, calls=%fused_computation.186 | loop fusion | bytes 25141248 | tf_op jit(solution)/shard_map/jit(_roll_static)/slice | solution.py:36
  35.3 13.1 %slice.204 = f32[32,5,8,1,1024]{4,3,2,1,0:T(1,128)} slice(f32[32,6,8,1,1024]{4,3,2,1,0:T(1,128)} %param.7), slice={[0:32], [1:6], [0:8], [0:1], [0:1024]} | slice | bytes 10485760 | tf_op jit(solution)/shard_map/jit(_roll_static)/slice | solution.py:44
  48.4 3.9 copy.324
  54.2 1.6 copy.320
  56.3 4.2 copy.323
  60.5 2.4 fusion.109
  63.0 6.6 %pad_maximum_fusion.8 = (f32[32,6,8,1,1024]{4,2,3,1,0:T(8,128)S(1)}, f32[32,6,8,1,1024]{4,2,3,1,0:T(8,128)}) fusion(f32[32,6,8,1,1]{4,2,3,1,0:T(8,128)S(1)} %bitcast.105, f32[32,6,8,1,1023]{4,2,3,1,0:T(8,128)S(1)} %copy.320, f32[32,6,8,1,1023]{4,2,3,1,0:T(8,128)} %copy.323, f32[32,6,8,1,1]{4,2,3,1,0:T(8,128)S(1)} %bitcast.106), kind=kLoop, calls=%fused_computation.46 | loop fusion | flops 3145728 | bytes 25165824 | tf_op jit(solution)/shard_map/jit(_roll_static)/concatenate | solution.py:36
  69.6 20.5 %fusion.36 = f32[32,6,8,1,1024]{4,0,3,2,1:T(8,128)S(1)} fusion(f32[32,6,8,1,1024]{4,0,3,2,1:T(8,128)S(1)} %bitcast.97, f32[32,6,1,1,1024]{4,0,3,2,1:T(8,128)} %collective-permute-done.1, f32[32,6,1,1,1024]{4,0,3,2,1:T(8,128)} %collective-permute-done, f32[32,6,8,1,1024]{4,2,3,1,0:T(8,128)S(1)} %pad_maximum_fusion.10, ...), kind=kLoop, calls=%fused_computation.44 | loop fusion | flops 26738688 | bytes 33030912 | tf_op jit(solution)/shard_map/add | solution.py:40
  90.1 1.4 fusion.107
  92.8 5.2 %collective-permute-start.3 = (f32[32,6,1,1,1024]{4,0,3,2,1:T(8,128)}, f32[32,6,1,1,1024]{4,0,3,2,1:T(8,128)}, u32[]{:S(2)}, u32[]{:S(2)}) collective-permute-start(f32[32,6,1,1,1024]{4,0,3,2,1:T(8,128)} %get-tuple-element.19), channel_id=1, source_target_pairs={{0,1},{1,2},{2,3},{3,4},{4,5},{5,6},{6,7},{7,8},{8,9},{9,10},{10,1... | collective-permute-start | bytes 2359304 | tf_op jit(solution)/shard_map/ppermute | solution.py:24
  98.0 1.4 fusion.106
  99.4 2.7 slice.264
  103.2 6.7 %fusion.105 = (f32[32,6,8,1,1023]{4,0,3,2,1:T(8,128)}, f32[32,6,8,1,1023]{4,0,3,2,1:T(8,128)}) fusion(f32[32,6,8,1,1024]{4,0,3,2,1:T(8,128)S(1)} %fusion.36), kind=kLoop, calls=%fused_computation.183 | loop fusion | bytes 25141248 | tf_op jit(solution)/shard_map/jit(_roll_static)/slice | solution.py:36
  109.9 14.1 %fusion.27 = f32[32,6,8,1,1024]{4,0,3,2,1:T(8,128)S(1)} fusion(f32[32,6,8,1,1024]{4,0,3,2,1:T(8,128)} %copy-done, f32[32,6,1,1,1024]{4,0,3,2,1:T(8,128)} %collective-permute-done.3, f32[32,6,1,1,1024]{4,0,3,2,1:T(8,128)} %collective-permute-done.2, f32[32,1,8,1,1024]{4,0,3,2,1:T(8,128)} %slice.265, f32[32,5,8,1,1024]{4,0,3,2,1:T(8,128)} %slice.264, ...), kind=kLoop, calls=%fused_computation.33 | loop fusion | flops 31457280 | bytes 33030912 | tf_op jit(solution)/shard_map/add | solution.py:40
  126.5 10.0 %collective-permute-start.5 = (f32[32,6,1,1,1024]{4,0,3,2,1:T(8,128)}, f32[32,6,1,1,1024]{4,0,3,2,1:T(8,128)}, u32[]{:S(2)}, u32[]{:S(2)}) collective-permute-start(f32[32,6,1,1,1024]{4,0,3,2,1:T(8,128)} %get-tuple-element.13), channel_id=1, source_target_pairs={{0,1},{1,2},{2,3},{3,4},{4,5},{5,6},{6,7},{7,8},{8,9},{9,10},{10,1... | collective-permute-start | bytes 2359304 | tf_op jit(solution)/shard_map/ppermute | solution.py:24
  136.5 1.5 fusion.103
  138.0 2.7 slice.272
  141.8 6.7 %fusion.102 = (f32[32,6,8,1,1023]{4,0,3,2,1:T(8,128)}, f32[32,6,8,1,1023]{4,0,3,2,1:T(8,128)}) fusion(f32[32,6,8,1,1024]{4,0,3,2,1:T(8,128)S(1)} %fusion.27), kind=kLoop, calls=%fused_computation.180 | loop fusion | bytes 25141248 | tf_op jit(solution)/shard_map/jit(_roll_static)/slice | solution.py:36
  148.4 9.7 %fusion.18 = f32[32,6,8,1,1024]{4,0,3,2,1:T(8,128)S(1)} fusion(f32[32,6,8,1,1024]{4,0,3,2,1:T(8,128)S(1)} %fusion.27, f32[32,6,1,1,1024]{4,0,3,2,1:T(8,128)} %collective-permute-done.5, f32[32,6,1,1,1024]{4,0,3,2,1:T(8,128)} %collective-permute-done.4, f32[32,1,8,1,1024]{4,0,3,2,1:T(8,128)} %slice.273, f32[32,5,8,1,1024]{4,0,3,2,1:T(8,128)} %slice.272, ...), kind=kLoop, calls=%fused_computation.22 | loop fusion | flops 31457280 | bytes 33030912 | tf_op jit(solution)/shard_map/add | solution.py:40
  160.7 5.0 %collective-permute-start.7 = (f32[32,6,1,1,1024]{4,0,3,2,1:T(8,128)}, f32[32,6,1,1,1024]{4,0,3,2,1:T(8,128)}, u32[]{:S(2)}, u32[]{:S(2)}) collective-permute-start(f32[32,6,1,1,1024]{4,0,3,2,1:T(8,128)} %get-tuple-element.7), channel_id=1, source_target_pairs={{0,1},{1,2},{2,3},{3,4},{4,5},{5,6},{6,7},{7,8},{8,9},{9,10},{10,1... | collective-permute-start | bytes 2359304 | tf_op jit(solution)/shard_map/ppermute | solution.py:24
  165.8 1.5 fusion.100
  167.2 11.2 %fusion.99 = (f32[32,6,8,1,1023]{4,0,3,2,1:T(8,128)}, f32[32,6,8,1,1023]{4,0,3,2,1:T(8,128)}) fusion(f32[32,6,8,1,1024]{4,0,3,2,1:T(8,128)} %copy-done.1), kind=kLoop, calls=%fused_computation.177 | loop fusion | bytes 25141248 | tf_op jit(solution)/shard_map/jit(_roll_static)/slice | solution.py:36
  178.5 13.5 %fusion.9 = bf16[32,6,8,1,1024]{4,0,3,2,1:T(8,128)(2,1)} fusion(f32[32,6,8,1,1024]{4,0,3,2,1:T(8,128)} %copy-done.1, f32[32,6,1,1,1024]{4,0,3,2,1:T(8,128)} %collective-permute-done.7, f32[32,6,1,1,1024]{4,0,3,2,1:T(8,128)} %collective-permute-done.6, f32[32,1,8,1,1024]{4,0,3,2,1:T(8,128)S(1)} %slice-done.1, f32[32,5,8,1,1024]{4,0,3,2,1:T(8,128)S(1)} %slice-done, ...), kind=kLoop, calls=%fused_computation.11 | loop fusion | flops 33030144 | bytes 29885184 | tf_op jit(solution)/shard_map/convert_element_type | solution.py:57
  191.9 14.4 %copy.289 = bf16[32,6,8,1,1024]{0,2,3,1,4:T(8,128)(2,1)} copy(bf16[32,6,8,1,1024]{4,0,3,2,1:T(8,128)(2,1)} %fusion.9) | data formatting | bytes 6291456 | tf_op jit(solution)/shard_map/convert_element_type | solution.py:57
  206.3 19.7 %reshape.582 = bf16[2,2,393216]{2,1,0:T(2,128)(2,1)} reshape(bf16[1024,6,1,8,32]{4,3,2,1,0:T(8,128)(2,1)} %bitcast.94) | data formatting | bytes 6291456
  226.0 4.5 all-to-all-start
  231.3 33.9 %all-to-all-done = bf16[2,2,393216]{2,1,0:T(2,128)(2,1)S(1)} async-done(((bf16[2,2,393216]{2,1,0:T(2,128)(2,1)}), bf16[2,2,393216]{2,1,0:T(2,128)(2,1)S(1)}, u32[]{:S(2)}, u32[]{:S(2)}) %all-to-all-start) | async-done | bytes 3145760 | tf_op jit(solution)/shard_map/all_to_all | solution.py:58
  265.2 11.1 %reshape.583 = bf16[1024,6,1,8,32]{4,3,2,1,0:T(8,128)(2,1)} reshape(bf16[2,2,393216]{2,1,0:T(2,128)(2,1)S(1)} %all-to-all-done) | data formatting | bytes 6291456
  276.2 14.0 %copy.290 = bf16[32,6,8,1,1024]{4,2,3,1,0:T(8,128)(2,1)S(1)} copy(bf16[32,6,8,1,1024]{0,2,3,1,4:T(8,128)(2,1)} %bitcast.95) | data formatting | bytes 6291456 | tf_op jit(solution)/shard_map/all_to_all | solution.py:58
  290.2 7.2 %reshape.563 = f32[32,6,8,1,2,512]{5,4,2,1,0,3:T(2,128)} reshape(bf16[32,6,8,1,1024]{4,2,3,1,0:T(8,128)(2,1)S(1)} %copy.290) | data formatting | bytes 9437184 | tf_op jit(solution)/shard_map/convert_element_type | solution.py:61
  297.4 6.6 %copy.296 = f32[2,32,6,8,1,512]{5,3,2,1,0,4:T(8,128)} copy(f32[2,32,6,8,1,512]{5,0,3,2,1,4:T(2,128)} %bitcast.98) | data formatting | bytes 12582912 | tf_op jit(solution)/shard_map/convert_element_type | solution.py:61
  304.0 9.7 %copy.297 = f32[64,6,8,1,512]{0,4,3,2,1:T(8,128)} copy(f32[64,6,8,1,512]{4,2,1,0,3:T(8,128)} %bitcast.93) | data formatting | bytes 12582912 | tf_op jit(solution)/shard_map/convert_element_type | solution.py:61
  313.7 16.2 %gather_fusion = f32[1024,64]{1,0:T(8,128)} fusion(f32[64,6,8,1,512]{0,4,3,2,1:T(8,128)} %copy.297, s32[1024]{0:T(1024)S(1)} %fusion.84), kind=kCustom, calls=%fused_computation | custom fusion | bytes 540672 | tf_op jit(solution)/shard_map/gather | solution.py:74
  333.4 4.5 collective-permute-start.8
  337.8 1.5 collective-permute-start.9
  340.6 3.5 copy.319
  344.1 2.9 reduce_sum.54
  347.6 3.6 bitcast_subtract_fusion
  352.5 1.4 fusion.50
  361.5 8.8 %fusion.37 = bf16[64,6,8,1,512]{4,0,1,2,3:T(8,128)(2,1)S(1)} fusion(f32[6,8,512]{2,0,1:T(8,128)S(1)} %copy.293, f32[64,6,8,512]{3,2,1,0:T(8,128)S(1)} %bitcast_subtract_fusion, f32[8,64,64]{2,1,0:T(8,128)S(1)} %fusion.117, f32[8,64]{1,0:T(8,128)S(1)} %broadcast_divide_fusion, f32[8]{0:T(128)S(1)} %get-tuple-element.30), kind=kOutput, calls=%fused_computation.59 | convolution fusion | flops 1211203584 | bytes 9668640 | tf_op jit(solution)/shard_map/jfrlc,rje->efrlc/dot_general | solution.py:102
  370.3 3.4 copy.305
  373.7 3.9 all-to-all-start.1
  377.7 36.6 %all-gather = f32[2,32,12]{1,2,0:T(8,128)S(1)} all-gather(f32[1,32,12]{1,2,0:T(8,128)S(1)} %bitcast.109), channel_id=1, replica_groups=mesh['member'=2,'slab'=16] {'member'}, dimensions={0}, use_global_device_ids=true | all-gather | bytes 4608 | tf_op jit(solution)/shard_map/all_gather | solution.py:105
  414.6 44.2 %psum.7 = f32[64,64]{1,0:T(8,128)S(1)} all-reduce(f32[64,64]{1,0:T(8,128)S(1)} %fusion.78), channel_id=1, replica_groups=mesh['member'=2,'slab'=16] {'member','slab'}, use_global_device_ids=true, to_apply=%region_6.7 | all-reduce | flops 4096 | bytes 32768 | tf_op jit(solution)/shard_map/psum | solution.py:111
  459.7 2.2 copy.306
  (124 shorter events, 29.2 us)
Async XLA Ops:
  0.6 15.8 %copy-start.2 = (f32[32,6,8,1,1024]{4,3,2,1,0:T(1,128)S(1)}, f32[32,6,8,1,1024]{4,3,2,1,0:T(1,128)}, u32[]{:S(2)}) copy-start(f32[32,6,8,1,1024]{4,3,2,1,0:T(1,128)} %param.7) | copy-start | bytes 18874372
  7.2 2.7 copy-start.3
  11.1 58.5 %collective-permute-start = (f32[32,6,1,1,1024]{4,0,3,2,1:T(8,128)}, f32[32,6,1,1,1024]{4,0,3,2,1:T(8,128)}, u32[]{:S(2)}, u32[]{:S(2)}) collective-permute-start(f32[32,6,1,1,1024]{4,0,3,2,1:T(8,128)} %get-tuple-element.24), channel_id=1, source_target_pairs={{1,0},{2,1},{3,2},{4,3},{5,4},{6,5},{7,6},{8,7},{9,8},{10,9},{11,1... | collective-permute-start | bytes 2359304 | tf_op jit(solution)/shard_map/ppermute | solution.py:27
  12.4 57.2 %collective-permute-start.1 = (f32[32,6,1,1,1024]{4,0,3,2,1:T(8,128)}, f32[32,6,1,1,1024]{4,0,3,2,1:T(8,128)}, u32[]{:S(2)}, u32[]{:S(2)}) collective-permute-start(f32[32,6,1,1,1024]{4,0,3,2,1:T(8,128)} %get-tuple-element.25), channel_id=1, source_target_pairs={{0,1},{1,2},{2,3},{3,4},{4,5},{5,6},{6,7},{7,8},{8,9},{9,10},{10,1... | collective-permute-start | bytes 2359304 | tf_op jit(solution)/shard_map/ppermute | solution.py:24
  48.4 4.0 slice-start.4
  48.4 5.5 %slice-start.9 = ((s8[6291456]{0:T(1024)(128)(4,1)}), s8[4194304]{0:T(1024)(128)(4,1)S(1)}, s32[]{:S(2)}) async-start(s8[6291456]{0:T(1024)(128)(4,1)} %bitcast.101), calls=%async_computation.11 | async-start | bytes 8388608
  52.6 1.2 copy-start.8
  52.6 1.1 copy-start.12
  52.6 1.6 slice-start.10
  52.7 3.2 slice-start.7
  53.8 2.5 slice-start.8
  54.2 6.3 %slice-start.2 = ((s8[6291456]{0:T(1024)(128)(4,1)}), s8[4194304]{0:T(1024)(128)(4,1)S(1)}, s32[]{:S(2)}) async-start(s8[6291456]{0:T(1024)(128)(4,1)} %bitcast.91), calls=%async_computation.4 | async-start | bytes 8388608
  55.9 4.7 %slice-start.3 = ((s8[6291456]{0:T(1024)(128)(4,1)}), s8[2097152]{0:T(1024)(128)(4,1)S(1)}, s32[]{:S(2)}) async-start(s8[6291456]{0:T(1024)(128)(4,1)} %bitcast.91), calls=%async_computation.5 | async-start | bytes 4194304
  60.5 9.0 %slice-start.5 = ((s8[6291456]{0:T(1024)(128)(4,1)}), s8[2097152]{0:T(1024)(128)(4,1)S(1)}, s32[]{:S(2)}) async-start(s8[6291456]{0:T(1024)(128)(4,1)} %bitcast.96), calls=%async_computation.7 | async-start | bytes 4194304
  63.0 6.6 %slice-start.6 = ((s8[6291456]{0:T(1024)(128)(4,1)}), s8[4194304]{0:T(1024)(128)(4,1)S(1)}, s32[]{:S(2)}) async-start(s8[6291456]{0:T(1024)(128)(4,1)} %bitcast.96), calls=%async_computation.8 | async-start | bytes 8388608
  90.1 13.1 %copy-start = (f32[32,6,8,1,1024]{4,0,3,2,1:T(8,128)}, f32[32,6,8,1,1024]{4,0,3,2,1:T(8,128)S(1)}, u32[]{:S(2)}) copy-start(f32[32,6,8,1,1024]{4,0,3,2,1:T(8,128)S(1)} %fusion.36) | copy-start | bytes 18874372
  91.5 18.4 %collective-permute-start.2 = (f32[32,6,1,1,1024]{4,0,3,2,1:T(8,128)}, f32[32,6,1,1,1024]{4,0,3,2,1:T(8,128)}, u32[]{:S(2)}, u32[]{:S(2)}) collective-permute-start(f32[32,6,1,1,1024]{4,0,3,2,1:T(8,128)} %get-tuple-element.18), channel_id=1, source_target_pairs={{1,0},{2,1},{3,2},{4,3},{5,4},{6,5},{7,6},{8,7},{9,8},{10,9},{11,1... | collective-permute-start | bytes 2359304 | tf_op jit(solution)/shard_map/ppermute | solution.py:27
  92.8 17.2 %collective-permute-start.3 = (f32[32,6,1,1,1024]{4,0,3,2,1:T(8,128)}, f32[32,6,1,1,1024]{4,0,3,2,1:T(8,128)}, u32[]{:S(2)}, u32[]{:S(2)}) collective-permute-start(f32[32,6,1,1,1024]{4,0,3,2,1:T(8,128)} %get-tuple-element.19), channel_id=1, source_target_pairs={{0,1},{1,2},{2,3},{3,4},{4,5},{5,6},{6,7},{7,8},{8,9},{9,10},{10,1... | collective-permute-start | bytes 2359304 | tf_op jit(solution)/shard_map/ppermute | solution.py:24
  125.2 23.2 %collective-permute-start.4 = (f32[32,6,1,1,1024]{4,0,3,2,1:T(8,128)}, f32[32,6,1,1,1024]{4,0,3,2,1:T(8,128)}, u32[]{:S(2)}, u32[]{:S(2)}) collective-permute-start(f32[32,6,1,1,1024]{4,0,3,2,1:T(8,128)} %get-tuple-element.12), channel_id=1, source_target_pairs={{1,0},{2,1},{3,2},{4,3},{5,4},{6,5},{7,6},{8,7},{9,8},{10,9},{11,1... | collective-permute-start | bytes 2359304 | tf_op jit(solution)/shard_map/ppermute | solution.py:27
  126.5 21.9 %collective-permute-start.5 = (f32[32,6,1,1,1024]{4,0,3,2,1:T(8,128)}, f32[32,6,1,1,1024]{4,0,3,2,1:T(8,128)}, u32[]{:S(2)}, u32[]{:S(2)}) collective-permute-start(f32[32,6,1,1,1024]{4,0,3,2,1:T(8,128)} %get-tuple-element.13), channel_id=1, source_target_pairs={{0,1},{1,2},{2,3},{3,4},{4,5},{5,6},{6,7},{7,8},{8,9},{9,10},{10,1... | collective-permute-start | bytes 2359304 | tf_op jit(solution)/shard_map/ppermute | solution.py:24
  158.1 9.1 %copy-start.1 = (f32[32,6,8,1,1024]{4,0,3,2,1:T(8,128)}, f32[32,6,8,1,1024]{4,0,3,2,1:T(8,128)S(1)}, u32[]{:S(2)}) copy-start(f32[32,6,8,1,1024]{4,0,3,2,1:T(8,128)S(1)} %fusion.18) | copy-start | bytes 18874372
  159.4 19.0 %collective-permute-start.6 = (f32[32,6,1,1,1024]{4,0,3,2,1:T(8,128)}, f32[32,6,1,1,1024]{4,0,3,2,1:T(8,128)}, u32[]{:S(2)}, u32[]{:S(2)}) collective-permute-start(f32[32,6,1,1,1024]{4,0,3,2,1:T(8,128)} %get-tuple-element.6), channel_id=1, source_target_pairs={{1,0},{2,1},{3,2},{4,3},{5,4},{6,5},{7,6},{8,7},{9,8},{10,9},{11,1... | collective-permute-start | bytes 2359304 | tf_op jit(solution)/shard_map/ppermute | solution.py:27
  160.7 17.7 %collective-permute-start.7 = (f32[32,6,1,1,1024]{4,0,3,2,1:T(8,128)}, f32[32,6,1,1,1024]{4,0,3,2,1:T(8,128)}, u32[]{:S(2)}, u32[]{:S(2)}) collective-permute-start(f32[32,6,1,1,1024]{4,0,3,2,1:T(8,128)} %get-tuple-element.7), channel_id=1, source_target_pairs={{0,1},{1,2},{2,3},{3,4},{4,5},{5,6},{6,7},{7,8},{8,9},{9,10},{10,1... | collective-permute-start | bytes 2359304 | tf_op jit(solution)/shard_map/ppermute | solution.py:24
  167.2 11.2 %slice-start = ((f32[32,6,8,1,1024]{4,0,3,2,1:T(8,128)}), f32[32,5,8,1,1024]{4,0,3,2,1:T(8,128)S(1)}, s32[]{:S(2)}) async-start(f32[32,6,8,1,1024]{4,0,3,2,1:T(8,128)} %copy-done.1), calls=%async_computation.2 | async-start | bytes 10485760 | tf_op jit(solution)/shard_map/jit(_roll_static)/slice | solution.py:44
  167.2 11.2 %slice-start.1 = ((f32[32,6,8,1,1024]{4,0,3,2,1:T(8,128)}), f32[32,1,8,1,1024]{4,0,3,2,1:T(8,128)S(1)}, s32[]{:S(2)}) async-start(f32[32,6,8,1,1024]{4,0,3,2,1:T(8,128)} %copy-done.1), calls=%async_computation.3 | async-start | bytes 2097152 | tf_op jit(solution)/shard_map/jit(_roll_static)/slice | solution.py:44
  226.0 4.7 %copy-start.15 = (s32[8]{0:T(128)S(1)}, s32[8]{0:T(128)}, u32[]{:S(2)}) copy-start(s32[8]{0:T(128)} %param.13) | copy-start | bytes 100
  226.0 5.2 %copy-start.11 = (s32[8,1,128]{2,1,0:T(1,128)S(1)}, s32[8,1,128]{2,1,0:T(1,128)}, u32[]{:S(2)}) copy-start(s32[8,1,128]{2,1,0:T(1,128)} %param.10) | copy-start | bytes 12292
  226.0 39.2 %all-to-all-start = ((bf16[2,2,393216]{2,1,0:T(2,128)(2,1)}), bf16[2,2,393216]{2,1,0:T(2,128)(2,1)S(1)}, u32[]{:S(2)}, u32[]{:S(2)}) async-start(bf16[2,2,393216]{2,1,0:T(2,128)(2,1)} %reshape.582), calls=%async_computation | async-start | bytes 6291456 | tf_op jit(solution)/shard_map/all_to_all | solution.py:58
  304.0 27.2 %copy-start.9 = (f32[8,1,128]{2,1,0:T(1,128)S(1)}, f32[8,1,128]{2,1,0:T(1,128)}, u32[]{:S(2)}) copy-start(f32[8,1,128]{2,1,0:T(1,128)} %param.12) | copy-start | bytes 12292
  304.0 27.2 %copy-start.10 = (f32[8,1,128]{2,1,0:T(1,128)S(1)}, f32[8,1,128]{2,1,0:T(1,128)}, u32[]{:S(2)}) copy-start(f32[8,1,128]{2,1,0:T(1,128)} %param.11) | copy-start | bytes 12292
  331.8 0.7 copy-start.4
  332.5 0.9 copy-start.6
  333.4 17.9 %collective-permute-start.8 = (f32[8,65,64]{1,2,0:T(8,128)}, f32[8,65,64]{1,2,0:T(8,128)S(1)}, u32[]{:S(2)}, u32[]{:S(2)}) collective-permute-start(f32[8,65,64]{1,2,0:T(8,128)} %pad_maximum_fusion.18), channel_id=1, source_target_pairs={{0,1},{1,2},{2,3},{3,4},{4,5},{5,6},{6,7},{7,8},{8,9},{9,10},{10,1... | collective-permute-start | bytes 399368 | tf_op jit(solution)/shard_map/ppermute | solution.py:24
  337.8 13.4 %collective-permute-start.9 = (f32[8,65,64]{1,2,0:T(8,128)}, f32[8,65,64]{1,2,0:T(8,128)}, u32[]{:S(2)}, u32[]{:S(2)}) collective-permute-start(f32[8,65,64]{1,2,0:T(8,128)} %pad_maximum_fusion.18), channel_id=1, source_target_pairs={{1,0},{2,1},{3,2},{4,3},{5,4},{6,5},{7,6},{8,7},{9,8},{10,9},{11,1... | collective-permute-start | bytes 399368 | tf_op jit(solution)/shard_map/ppermute | solution.py:27
  347.5 3.8 copy-start.5
  347.5 3.8 copy-start.7
  347.5 4.9 %copy-start.13 = (f32[8]{0:T(128)S(1)}, f32[8]{0:T(128)}, u32[]{:S(2)}) copy-start(f32[8]{0:T(128)} %get-tuple-element.39) | copy-start | bytes 100
  347.6 4.9 %copy-start.14 = (f32[8]{0:T(128)S(1)}, f32[8]{0:T(128)}, u32[]{:S(2)}) copy-start(f32[8]{0:T(128)} %get-tuple-element.40) | copy-start | bytes 100
  373.7 86.0 %all-to-all-start.1 = ((bf16[64,6,8,1,512]{4,2,3,1,0:T(8,128)(2,1)}), bf16[64,6,8,1,512]{4,2,3,1,0:T(8,128)(2,1)S(1)}, u32[]{:S(2)}, u32[]{:S(2)}) async-start(bf16[64,6,8,1,512]{4,2,3,1,0:T(8,128)(2,1)} %copy.305), calls=%async_computation.1 | async-start | bytes 6291456 | tf_op jit(solution)/shard_map/all_to_all | solution.py:104
where the time goes:
time: 468 us; the launch traced here: 462 us
  local copies, waits for them, and re-layouts  207 us (44%)
  blocking collectives  80.8 us (17%)
  other arithmetic  77.7 us (17%)
  starting transfers between devices  43.7 us (9%)
  waiting for transfers between devices  33.9 us (7%)
  matrix products  17.6 us (4%)
    unnamed x57, local copies, waits for them, and re-layouts  54.7 us
    slice x8, local copies, waits for them, and re-layouts, advance(): right_col = jnp.roll(middle, -1, 4)  50.3 us
    psum x1, blocking collectives, body(): summed = lax.psum(weight_rows, ('member', 'slab')) / regions  44.2 us
    add x3, other arithmetic, advance(): middle + diffusion * laplace - advection * (right_col - left_col)  44.2 us
    all_gather x1, blocking collectives, body(): every_param = lax.all_gather(params, 'member', axis=0, tiled=True)  36.6 us
    all_to_all x1, waiting for transfers between devices, body(): lax.all_to_all(propagate_timestep, 'member', split_axis=4, concat_axis=0,...  33.9 us
    ppermute x5, starting transfers between devices, with_halo(): lax.ppermute(lax.slice_in_dim(block, block.shape[dim] - width, None, axis...  28.7 us
    convert_element_type x3, local copies, waits for them, and re-layouts, body(): xfull = latitude_band.astype(jnp.float32)  23.5 us
  transfers between devices with their start and end apart: 12, of which 1 were waited for; matrix products, arithmetic and copies ran while one was open for 22% of the time, Pallas kernels for 0%

commit v1 on v0

v1 whole, which is shorter than its diff:
```python
import math

import jax
import jax.numpy as jnp
from jax import lax
from jax.experimental import pallas as pl
from jax.experimental.pallas import tpu as pltpu
from jax.sharding import PartitionSpec as P


HALO = 8
STEPS = 4
NS_STEPS = 5
LANES = 128
TILE = 8

diffusion = 0.2
advection = 0.15
vertical = 0.1
coupling = 0.2


def planes_of(fields, levels):
    return [(f, l) for f in range(fields) for l in range(levels)]


def pack_kernel(fields, rows, levels, cols, count, odd_ref, x_ref, *rest):
    outs, turned, edges, sems = rest[:2 * count + 1], *rest[2 * count + 1:]
    groups = cols // LANES
    stride = fields * rows * levels * groups
    planes = fields * levels
    tile = pl.program_id(0)

    def row(y, _):
        for p, (f, l) in enumerate(planes_of(fields, levels)):
            for s in range(groups):
                start = ((f * rows + y) * levels + l) * groups + s
                turned[tile, p, y, :, s * LANES:(s + 1) * LANES] = x_ref[pl.ds(start, TILE, stride=stride), :]
        return 0

    lax.fori_loop(0, rows, row, 0)

    def edge(y, _):
        for side in range(2):
            at = jnp.where(odd_ref[0] == side, rows - STEPS, 0) + y
            for p in range(planes):
                edges[tile, side, p, y] = turned[tile, p, at].astype(jnp.bfloat16)
        return 0

    lax.fori_loop(0, STEPS, edge, 0)

    def copies(k):
        pairs = [(edges.at[k, 0], outs[2 * k]), (edges.at[k, 1], outs[2 * k + 1]), (turned.at[k], outs[-1].at[k])]
        return [pltpu.make_async_copy(src, dst, sems.at[k, i]) for i, (src, dst) in enumerate(pairs)]

    for k in range(count):
        @pl.when(tile == k)
        def _():
            for copy in copies(k):
                copy.start()

    @pl.when(tile == count - 1)
    def _():
        for k in range(count):
            for copy in copies(k):
                copy.wait()


def pack(odd, x2, first, count, fields, rows, levels, cols):
    planes = fields * levels
    block = TILE * fields * rows * levels * cols // LANES
    edge = (planes, STEPS, TILE, cols)
    turned = (count, planes, rows, TILE, cols)
    return pl.pallas_call(
        lambda *refs: pack_kernel(fields, rows, levels, cols, count, *refs),
        grid=(count,),
        in_specs=[pl.BlockSpec(memory_space=pltpu.SMEM), pl.BlockSpec((block, LANES), lambda i: (first + i, 0))],
        out_specs=[pl.BlockSpec(memory_space=pl.ANY)] * (2 * count + 1),
        out_shape=[jax.ShapeDtypeStruct(edge, jnp.bfloat16)] * (2 * count) + [jax.ShapeDtypeStruct(turned, jnp.float32)],
        scratch_shapes=[
            pltpu.VMEM(turned, jnp.float32),
            pltpu.VMEM((count, 2, *edge), jnp.bfloat16),
            pltpu.SemaphoreType.DMA((count, 3)),
        ],
        name="pack",
    )(odd, x2)


def stencil_kernel(fields, rows, levels, cols, blocks, splits, local, odd_ref, open_ref, x_ref, first_ref, second_ref, coef_ref, cell_ref, *rest):
    out_refs = rest[:len(splits)]
    obs_ref = rest[len(splits)]
    *state, mixed, sem = rest[len(splits) + 1:]
    groups = cols // LANES
    block_cols = cols // blocks
    pairs = planes_of(fields, levels)
    planes = len(pairs)

    own_copy = pltpu.make_async_copy(x_ref.at[local], state[0].at[:, pl.ds(STEPS, rows)], sem)
    own_copy.start()

    def tile_at(s):
        return slice(s * LANES, (s + 1) * LANES)

    odd = odd_ref[0] == 1

    def load_edge(y, _):
        for p in range(planes):
            first = first_ref[p, y].astype(jnp.float32)
            second = second_ref[p, y].astype(jnp.float32)
            state[0][p, y] = jnp.where(odd, first, second)
            state[0][p, STEPS + rows + y] = jnp.where(odd, second, first)
        return 0

    lax.fori_loop(0, STEPS, load_edge, 0)
    own_copy.wait()

    lane = lax.broadcasted_iota(jnp.int32, (TILE, LANES), 1)
    at_last = lane == LANES - 1
    at_first = lane == 0
    centre = (1.0 - 4.0 * diffusion - vertical) / diffusion
    below_part = vertical / diffusion
    right_part = (diffusion - advection) / diffusion
    left_part = (diffusion + advection) / diffusion
    next_part = coupling / diffusion
    scale = diffusion ** STEPS
    coefs = [next_part * coef_ref[0, f] for f in range(fields)]

    def rest_of_step(src, y, p):
        f, l = pairs[p]
        after = ((f + 1) % fields) * levels + l
        under = f * levels + (l - 1) % levels
        mid, out = [], []
        for s in range(groups):
            here = src[p, y, :, tile_at(s)]
            around = src[p, y + 1, :, tile_at(s)] + src[p, y - 1, :, tile_at(s)]
            if under == p:
                whole = centre + below_part
                own = here if abs(whole - 1.0) < 1e-12 else whole * here
            else:
                own = centre * here + below_part * src[under, y, :, tile_at(s)]
            mid.append(here)
            out.append((around + own) + coefs[f] * src[after, y, :, tile_at(s)])
        return mid, out

    pace = 2 if rows % 2 == 0 else 1
    for t in range(1, STEPS + 1):
        src, dst = state[(t - 1) % 2], state[t % 2]
        reach = STEPS - t
        ratio = math.comb(STEPS, t - 1) / math.comb(STEPS, t)

        def edge_rows(i, _):
            for side, y in enumerate((t + i, STEPS + rows + i)):
                for p in range(planes):
                    for s, value in enumerate(rest_of_step(src, y, p)[1]):
                        dst[p, y, :, tile_at(s)] = value * open_ref[side]
            return 0

        def own_rows(i, _):
            for k in range(pace):
                mine = pace * i + k
                for p in range(planes):
                    mid, out = rest_of_step(src, STEPS + mine, p)
                    if t > 1:
                        mid = [mixed[p, mine, :, tile_at(s)] for s in range(groups)]
                    ahead = [pltpu.roll(v, LANES - 1, 1) for v in mid]
                    behind = [pltpu.roll(v, 1, 1) for v in mid]
                    for s in range(groups):
                        right = jnp.where(at_last, ahead[(s + 1) % groups], ahead[s])
                        left = jnp.where(at_first, behind[(s - 1) % groups], behind[s])
                        value = out[s] + (ratio * right_part * right + ratio * left_part * left)
                        if t < STEPS:
                            dst[p, STEPS + mine, :, tile_at(s)] = out[s]
                            mixed[p, mine, :, tile_at(s)] = value
                            continue
                        value = value * scale
                        mixed[p, mine, :, tile_at(s)] = value
                        for g, (start, count) in enumerate(splits):
                            if start <= p < start + count:
                                at = pl.ds(pl.multiple_of(mine * TILE, TILE), TILE)
                                out_refs[g][p - start, s, at, :] = value.astype(jnp.bfloat16)
            return 0

        if reach:
            lax.fori_loop(0, reach, edge_rows, 0)
        lax.fori_loop(0, rows // pace, own_rows, 0)

    column = lax.broadcasted_iota(jnp.int32, (block_cols, LANES), 0)

    def observe(i, _):
        for k in range(pace):
            y = pace * i + k
            for b in range(blocks):
                cell = cell_ref[y, b:b + 1, :]
                plane = cell // block_cols
                pick = jnp.where(column == cell - plane * block_cols, 1.0, 0.0).astype(jnp.bfloat16)
                part = mixed[:, y, :, b * block_cols:(b + 1) * block_cols]
                part = part.reshape(planes * TILE, block_cols).astype(jnp.bfloat16)
                found = jnp.dot(part, pick, preferred_element_type=jnp.float32).reshape(planes, TILE, LANES)
                total = jnp.zeros((TILE, LANES), jnp.float32)
                for p in range(planes):
                    total = jnp.where(plane == p, found[p], total)
                obs_ref[y, b] = total.astype(jnp.bfloat16)
        return 0

    lax.fori_loop(0, rows // pace, observe, 0)


def stencil(odd, inside, turned, first, second, coef, cells, tile, local, splits, fields, rows, levels, cols):
    planes = fields * levels
    blocks = cells.shape[1]
    outs = [jax.ShapeDtypeStruct((count, cols // LANES, rows * TILE, LANES), jnp.bfloat16) for _, count in splits]
    outs.append(jax.ShapeDtypeStruct((rows, blocks, TILE, LANES), jnp.bfloat16))
    room = pltpu.VMEM((planes, rows + 2 * STEPS, TILE, cols), jnp.float32)

    def all_of(shape):
        return pl.BlockSpec(shape, lambda i: (0,) * len(shape))

    return pl.pallas_call(
        lambda *refs: stencil_kernel(fields, rows, levels, cols, blocks, splits, local, *refs),
        grid=(1,),
        in_specs=[
            pl.BlockSpec(memory_space=pltpu.SMEM),
            pl.BlockSpec(memory_space=pltpu.SMEM),
            pl.BlockSpec(memory_space=pl.ANY),
            all_of(first.shape),
            all_of(second.shape),
            pl.BlockSpec((1, fields, TILE, LANES), lambda i: (tile, 0, 0, 0)),
            all_of(cells.shape),
        ],
        out_specs=[all_of(out.shape) for out in outs],
        out_shape=outs,
        scratch_shapes=[room, room, pltpu.VMEM((planes, rows, TILE, cols), jnp.float32), pltpu.SemaphoreType.DMA],
        name="stencil",
    )(odd, inside, turned, first, second, coef, cells)


def spread_kernel(members, rows, blocks, depth, w_ref, upper_ref, lower_ref):
    ensemble = w_ref.shape[2]
    member = lax.broadcasted_iota(jnp.int32, (ensemble, depth), 0)
    column = lax.broadcasted_iota(jnp.int32, (ensemble, depth), 1)
    place = jnp.where(member == column // (rows * TILE) * TILE + column % TILE, 1.0, 0.0).astype(jnp.bfloat16)
    mine = lax.broadcasted_iota(jnp.int32, (members * rows, depth), 0) % rows
    theirs = lax.broadcasted_iota(jnp.int32, (members * rows, depth), 1) // TILE % rows
    keep = mine == theirs
    for b in range(blocks):
        w = w_ref[b]
        high = w.astype(jnp.bfloat16)
        low = (w - high.astype(jnp.float32)).astype(jnp.bfloat16)
        for part, ref in ((high, upper_ref), (low, lower_ref)):
            wide = jnp.dot(part, place, preferred_element_type=jnp.float32)
            ref[b] = jnp.where(keep, wide, 0.0).astype(jnp.bfloat16)


def spread(w, members, rows):
    blocks, _, ensemble = w.shape
    depth = ensemble * rows
    out = jax.ShapeDtypeStruct((blocks, members * rows, depth), jnp.bfloat16)
    return pl.pallas_call(
        lambda *refs: spread_kernel(members, rows, blocks, depth, *refs),
        out_shape=[out, out],
        name="spread",
    )(w)


def update_kernel(members, rows, cols, blocks, count, upper, lower, *rest):
    pieces, out_ref = rest[:count], rest[-1]
    groups = cols // blocks // LANES
    for b in range(blocks):
        columns = []
        for s in range(b * groups, (b + 1) * groups):
            columns.append(jnp.concatenate([piece[0, s] for piece in pieces], axis=0))
        x = jnp.concatenate(columns, axis=1) if groups > 1 else columns[0]
        total = jnp.dot(upper[b], x, preferred_element_type=jnp.float32)
        total = total + jnp.dot(lower[b], x, preferred_element_type=jnp.float32)
        total = total.reshape(members, rows, groups * LANES).astype(jnp.bfloat16)
        out_ref[:, 0, :, b * groups * LANES:(b + 1) * groups * LANES] = total


def update(upper, lower, pieces, offsets, start, count, held, members, planes, rows, cols):
    blocks = upper.shape[0]

    def piece_spec(piece, offset):
        return pl.BlockSpec((1, *piece.shape[1:]), lambda i: (offset + i, 0, 0, 0))

    in_specs = [pl.BlockSpec(upper.shape, lambda i: (0, 0, 0))] * 2
    in_specs += [piece_spec(piece, offset) for piece, offset in zip(pieces, offsets)]
    args = [upper, lower, *pieces]
    aliases = {}
    if held is not None:
        aliases = {len(args): 0}
        in_specs.append(pl.BlockSpec(memory_space=pl.ANY))
        args.append(held)
    return pl.pallas_call(
        lambda *refs: update_kernel(members, rows, cols, blocks, len(pieces), *refs),
        grid=(count,),
        in_specs=in_specs,
        out_specs=pl.BlockSpec((members, 1, rows, cols), lambda i: (0, start + i, 0, 0)),
        out_shape=jax.ShapeDtypeStruct((members, planes, rows, cols), jnp.bfloat16),
        input_output_aliases=aliases,
        name="update",
    )(*args)


def from_member(array, shift):
    count = lax.axis_size("member")
    return lax.ppermute(array, "member", [((i + shift) % count, i) for i in range(count)])


def all_members(array):
    return [array] + [from_member(array, shift) for shift in range(1, lax.axis_size("member"))]


def swap_one(array):
    return lax.ppermute(array, "slab", [(i, i ^ 1) for i in range(lax.axis_size("slab"))])


def swap_two(array):
    pairs = [(i, i + 1) for i in range(1, lax.axis_size("slab") - 1, 2)]
    return lax.ppermute(array, "slab", pairs + [(j, i) for i, j in pairs])


def groups_of(planes):
    sizes = [2] * (planes // 2 - 1) + [1, 1] if planes % 2 == 0 else [1] * planes
    return [(sum(sizes[:i]), size) for i, size in enumerate(sizes)]


def cycle(prior_ensemble_fields, params, influence, obs_cell, obs_value, obs_prec, cutoff):
    highest = lax.Precision.HIGHEST
    fine_grain = lax.Precision.HIGH
    members, fields, rows, levels, cols = prior_ensemble_fields.shape
    planes = fields * levels
    tiles = members // TILE
    devices = lax.axis_size("member")
    slabs = lax.axis_size("slab")
    ensemble = members * devices
    me = lax.axis_index("member")
    place = lax.axis_index("slab")
    dims = (fields, rows, levels, cols)
    x2 = prior_ensemble_fields.reshape(members * fields * rows * levels * (cols // LANES), LANES)

    odd = (place % 2).astype(jnp.int32).reshape(1)

    *packed, turned = pack(odd, x2, 0, 1, *dims)
    turned = [(turned, 0)]
    if tiles > 1:
        *more, others = pack(odd, x2, 1, tiles - 1, *dims)
        packed += more
        turned += [(others, i) for i in range(tiles - 1)]
    edges = []
    for i in range(tiles):
        edges.append((swap_one(packed[2 * i]), swap_two(packed[2 * i + 1])))

    columns = obs_cell.shape[2]
    npar = params.shape[1]
    own_small = jnp.concatenate(
        [obs_cell[:, 0].astype(jnp.float32), obs_value[:, 0], obs_prec[:, 0]]
        + [jnp.pad(params.T, ((0, -npar % TILE), (0, columns - members)))]
    )
    small = jnp.stack(all_members(own_small))
    every_param = small[:, 3 * rows:3 * rows + npar, :members].transpose(0, 2, 1).reshape(ensemble, npar)
    every = jnp.concatenate([small[:, :3 * rows]] * 2)
    every = lax.dynamic_slice_in_dim(every, devices - me, devices, 0).reshape(devices, 3, rows, columns)
    cells = jnp.moveaxis(every[:, 0], 0, 1).astype(jnp.int32)
    values = jnp.moveaxis(every[:, 1], 0, 1)
    precs = jnp.moveaxis(every[:, 2], 0, 1)

    coef = jnp.dot(params, influence.astype(jnp.float32), precision=highest)
    coef = jnp.broadcast_to(coef.reshape(tiles, TILE, fields).transpose(0, 2, 1)[..., None], (tiles, fields, TILE, LANES))
    inside = jnp.stack([place > 0, place < slabs - 1]).astype(jnp.float32)

    fine = groups_of(planes)
    forecasts, observed = [], []
    for i in range(tiles):
        splits = fine if i == tiles - 1 else [(0, planes)]
        fields_here, local = turned[i]
        *outs, obs = stencil(odd, inside, fields_here, *edges[i], coef, cells, i, local, splits, *dims)
        forecasts.append(outs)
        observed.append(obs)
    ens_obs = jnp.stack(all_members(jnp.stack(observed)))
    sent = []
    for outs in forecasts:
        arrays = []
        for out in outs:
            arrays.append(all_members(out))
        sent.append(arrays)

    ens_obs = ens_obs.transpose(2, 3, 0, 1, 4, 5).reshape(rows, devices, ensemble, LANES).astype(jnp.float32)
    ybar = jnp.mean(ens_obs, axis=2, keepdims=True)
    ypert = ens_obs - ybar
    weighted = precs * (values - ybar[:, :, 0])
    gram = jnp.einsum("rbeo,rbfo->rbef", ypert * precs[:, :, None], ypert, precision=fine_grain)
    gvec = jnp.einsum("rbeo,rbo->rbe", ypert, weighted, precision=highest)
    stacked = jnp.concatenate([gram, gvec[:, :, None, :]], axis=2)
    stacked = jnp.concatenate([stacked[:, 0::2], stacked[:, 1::2]], axis=3)
    rounded = stacked.astype(jnp.bfloat16)
    near, far = swap_one(rounded), swap_two(rounded)
    near, far = near.astype(jnp.float32), far.astype(jnp.float32)
    is_odd = place % 2 == 1
    wide = jnp.concatenate([jnp.where(is_odd, near, far), stacked, jnp.where(is_odd, far, near)], axis=0)
    radius = cutoff.astype(jnp.float32)
    local = jnp.zeros_like(stacked)
    for offset in range(-HALO, HALO + 1):
        weight = jnp.maximum(0.0, 1.0 - abs(offset) / (radius + 1.0))
        local = local + weight[:, None, None, None] * wide[rows + offset:2 * rows + offset]
    local = jnp.stack([local[..., :ensemble], local[..., ensemble:]], axis=2).reshape(rows, devices, ensemble + 1, ensemble)
    gram_loc = local[:, :, :ensemble]
    gvec_loc = local[:, :, ensemble]
    eye_mat = jnp.eye(ensemble, dtype=jnp.float32)
    amat = (ensemble - 1.0) * eye_mat + gram_loc
    scale = jnp.sqrt(jnp.sum(amat * amat, axis=(2, 3)))[:, :, None, None]
    ymat = amat / scale
    zmat = None
    for _ in range(NS_STEPS):
        middle = 1.5 * eye_mat - 0.5 * (ymat if zmat is None else jnp.matmul(zmat, ymat, precision=fine_grain))
        ymat = jnp.matmul(ymat, middle, precision=fine_grain)
        zmat = middle if zmat is None else jnp.matmul(middle, zmat, precision=fine_grain)
    wpert = math.sqrt(ensemble - 1.0) * zmat / jnp.sqrt(scale)
    inner = jnp.matmul(zmat, gvec_loc[..., None], precision=highest)
    wbar = jnp.matmul(zmat, inner, precision=highest) / scale
    weights = (wpert + wbar)[..., :members]

    direct = weights + (1.0 - jnp.sum(weights, axis=2, keepdims=True)) / ensemble
    w = direct.transpose(1, 3, 0, 2).reshape(devices, members * rows, ensemble)

    upper, lower = spread(w, members, rows)

    analysis = None
    for g, (start, count) in enumerate(fine):
        pieces, offsets = [], []
        for r in range(devices):
            for arrays in sent:
                pieces.append(arrays[g if len(arrays) > 1 else 0][r])
                offsets.append(0 if len(arrays) > 1 else start)
        analysis = update(upper, lower, pieces, offsets, start, count, analysis, members, planes, rows, cols)
    analysis = analysis.reshape(members, fields, levels, rows, cols).transpose(0, 1, 3, 2, 4)

    pbar = jnp.mean(every_param, axis=0)
    ppert = every_param - pbar
    weight_rows = jnp.sum(weights, axis=(0, 1))
    part = jnp.einsum("jk,je->ke", ppert, weight_rows, precision=highest)
    step = 1
    while step < slabs:
        part = part + lax.ppermute(part, "slab", [(i, i ^ step) for i in range(slabs)])
        step *= 2
    total = part / (rows * slabs * devices)
    param_analysis = pbar + total.T
    return (analysis, param_analysis)


def solution(mesh):
    in_specs = (
        P("member", None, "slab", None, None),
        P("member", None),
        P(),
        P("slab", "member", None),
        P("slab", "member", None),
        P("slab", "member", None),
        P("slab"),
    )
    out_specs = (P("member", None, "slab", None, None), P("member", None))
    return jax.shard_map(cycle, mesh=mesh, in_specs=in_specs, out_specs=out_specs, check_vma=False)
```

time: 468 us -> 170 us (0.36)
  the two profiles are of different devices: /device:TPU:0 before, /device:TPU:10 now
where the time goes in v1:
time: 170 us; the launch traced here: 169 us
  Pallas kernels  63.9 us (38%)
  starting transfers between devices  36.4 us (21%)
  waiting for transfers between devices  35.8 us (21%)
  matrix products  16.2 us (10%)
  local copies, waits for them, and re-layouts  8.18 us (5%)
  other arithmetic  7.16 us (4%)
    pallas_call x4, Pallas kernels, stencil(): pl.pallas_call(lambda *refs: stencil_kernel(fields, rows, levels, cols, b...  35.9 us
    ppermute x9, waiting for transfers between devices, from_member(): lax.ppermute(array, 'member', [((i + shift) % count, i) for i in range(co...  26.8 us
    ppermute x5, starting transfers between devices, swap_two(): return lax.ppermute(array, 'slab', pairs + [(j, i) for i, j in pairs])  14.4 us
    pallas_call x4, Pallas kernels, update(): pl.pallas_call(lambda *refs: update_kernel(members, rows, cols, blocks, l...  14.1 us
    pallas_call x2, Pallas kernels, pack(): pl.pallas_call(lambda *refs: pack_kernel(fields, rows, levels, cols, coun...  11.6 us
    ppermute x4, starting transfers between devices, cycle(): lax.ppermute(part, 'slab', [(i, i ^ step) for i in range(slabs)])  10.2 us
    ppermute x9, starting transfers between devices, from_member(): lax.ppermute(array, 'member', [((i + shift) % count, i) for i in range(co...  7.88 us
    ppermute x4, waiting for transfers between devices, cycle(): lax.ppermute(part, 'slab', [(i, i ^ step) for i in range(slabs)])  7 us
  transfers between devices with their start and end apart: 23, of which 6 were waited for; matrix products, arithmetic and copies ran while one was open for 15% of the time, Pallas kernels for 26%

profile of v1, /device:TPU:10, one launch (start us, length us, event | category | flops | bytes accessed | tf_op | source)
XLA Modules:
  0.0 168.9 jit_solution(13523514096527918240)
XLA Ops:
  0.7 7.7 %pack.3 = (bf16[6,4,8,1024]{3,2,1,0:T(8,128)(2,1)}, bf16[6,4,8,1024]{3,2,1,0:T(8,128)(2,1)}, bf16[6,4,8,1024]{3,2,1,0:T(8,128)(2,1)}, bf16[6,4,8,1024]{3,2,1,0:T...) custom-call(s32[1]{0:T(128)} %bitcast.refs_0_, ...), custom_call_target="tpu_custom_call" | custom-call | tf_op jit(solution)/shard_map/pack/pallas_call | solution.py:74
  8.5 3.4 %collective-permute-start.4 = (bf16[6,4,8,1024]{3,2,1,0:T(8,128)(2,1)}, bf16[6,4,8,1024]{3,2,1,0:T(8,128)(2,1)S(1)}, u32[]{:S(2)}, u32[]{:S(2)}) collective-permute-start(bf16[6,4,8,1024]{3,2,1,0:T(8,128)(2,1)} %get-tuple-element.31), channel_id=1, source_target_pairs={{1,2},{3,4},{5,6},{7,8},{9,10},{11,12},{13,14},{2,1},{4,3},{6,5},{... | collective-permute-start | bytes 1179656 | tf_op jit(solution)/shard_map/ppermute | solution.py:319
  12.6 2.8 %collective-permute-start.6 = (bf16[6,4,8,1024]{3,2,1,0:T(8,128)(2,1)}, bf16[6,4,8,1024]{3,2,1,0:T(8,128)(2,1)S(1)}, u32[]{:S(2)}, u32[]{:S(2)}) collective-permute-start(bf16[6,4,8,1024]{3,2,1,0:T(8,128)(2,1)} %get-tuple-element.34), channel_id=1, source_target_pairs={{1,2},{3,4},{5,6},{7,8},{9,10},{11,12},{13,14},{2,1},{4,3},{6,5},{... | collective-permute-start | bytes 1179656 | tf_op jit(solution)/shard_map/ppermute | solution.py:319
  16.2 3.9 %pack.2 = (bf16[6,4,8,1024]{3,2,1,0:T(8,128)(2,1)}, bf16[6,4,8,1024]{3,2,1,0:T(8,128)(2,1)}, f32[1,6,8,8,1024]{4,3,2,1,0:T(8,128)}) custom-call(s32[1]{0:T(128)} %bitcast.refs_0_, f32[12288,128]{1,0:T(8,128)} %bitcast.99), custom_call_target="tpu_custom_call" | custom-call | tf_op jit(solution)/shard_map/pack/pallas_call | solution.py:74
  20.2 0.7 collective-permute-start
  20.9 3.1 %collective-permute-start.1 = (bf16[6,4,8,1024]{3,2,1,0:T(8,128)(2,1)}, bf16[6,4,8,1024]{3,2,1,0:T(8,128)(2,1)S(1)}, u32[]{:S(2)}, u32[]{:S(2)}) collective-permute-start(bf16[6,4,8,1024]{3,2,1,0:T(8,128)(2,1)} %get-tuple-element.27), channel_id=1, source_target_pairs={{1,2},{3,4},{5,6},{7,8},{9,10},{11,12},{13,14},{2,1},{4,3},{6,5},{... | collective-permute-start | bytes 1179656 | tf_op jit(solution)/shard_map/ppermute | solution.py:319
  24.0 3.0 %collective-permute-start.7 = (bf16[6,4,8,1024]{3,2,1,0:T(8,128)(2,1)}, bf16[6,4,8,1024]{3,2,1,0:T(8,128)(2,1)S(1)}, u32[]{:S(2)}, u32[]{:S(2)}) collective-permute-start(bf16[6,4,8,1024]{3,2,1,0:T(8,128)(2,1)} %get-tuple-element.36), channel_id=1, source_target_pairs={{0,1},{1,0},{2,3},{3,2},{4,5},{5,4},{6,7},{7,6},{8,9},{9,8},{10,11... | collective-permute-start | bytes 1179656 | tf_op jit(solution)/shard_map/ppermute | solution.py:314
  27.1 2.6 %collective-permute-start.8 = (bf16[6,4,8,1024]{3,2,1,0:T(8,128)(2,1)}, bf16[6,4,8,1024]{3,2,1,0:T(8,128)(2,1)S(1)}, u32[]{:S(2)}, u32[]{:S(2)}) collective-permute-start(bf16[6,4,8,1024]{3,2,1,0:T(8,128)(2,1)} %get-tuple-element.37), channel_id=1, source_target_pairs={{1,2},{3,4},{5,6},{7,8},{9,10},{11,12},{13,14},{2,1},{4,3},{6,5},{... | collective-permute-start | bytes 1179656 | tf_op jit(solution)/shard_map/ppermute | solution.py:319
  30.4 0.7 broadcast_in_dim.4.refs_5_
  31.1 9.0 %stencil.5 = (bf16[6,8,64,128]{3,2,1,0:T(8,128)(2,1)}, bf16[8,2,8,128]{3,2,1,0:T(8,128)(2,1)}) custom-call(s32[1]{0:T(128)} %bitcast.refs_0_, f32[2]{0:T(128)} %add_convert_fusion.refs_1_, f32[3,6,8,8,1024]{4,3,2,1,0:T(8,128)} %get-tuple-element.29.refs_2_, bf16[6,4,8,1024]{3,2,1,0:T(8,128)(2,1)} %copy-done.4, bf16[6,4,8,1024]{3,2,1,0:T(8,128)(2,1)} %copy-done.5, ...), custom_call_target="tpu_custom_call" | custom-call | tf_op jit(solution)/shard_map/stencil/pallas_call | solution.py:218
  40.1 0.8 copy-done.7
  40.9 8.9 %stencil.6 = (bf16[6,8,64,128]{3,2,1,0:T(8,128)(2,1)}, bf16[8,2,8,128]{3,2,1,0:T(8,128)(2,1)}) custom-call(s32[1]{0:T(128)} %bitcast.refs_0_, f32[2]{0:T(128)} %add_convert_fusion.refs_1_, f32[3,6,8,8,1024]{4,3,2,1,0:T(8,128)} %get-tuple-element.29.refs_2_, bf16[6,4,8,1024]{3,2,1,0:T(8,128)(2,1)} %copy-done.6, bf16[6,4,8,1024]{3,2,1,0:T(8,128)(2,1)} %copy-done.7, ...), custom_call_target="tpu_custom_call" | custom-call | tf_op jit(solution)/shard_map/stencil/pallas_call | solution.py:218
  49.9 0.8 copy-done.8
  50.6 0.7 copy-done.9
  51.4 9.0 %stencil.7 = (bf16[2,8,64,128]{3,2,1,0:T(8,128)(2,1)}, bf16[2,8,64,128]{3,2,1,0:T(8,128)(2,1)}, bf16[1,8,64,128]{3,2,1,0:T(8,128)(2,1)}, bf16[1,8,64,128]{3,2,1,0:T(8,128)(2,1)}, bf16[8,2,8,128]{3,2,1,0:T(8,128)(2,1)}) custom-call(s32[1]{0:T(128)} %bitcast.refs_0_, f32[2]{0:T(128)} %add_convert_fusion.refs_1_, ...), custom_call_target="tpu_custom_call" | custom-call | tf_op jit(solution)/shard_map/stencil/pallas_call | solution.py:218
  60.5 0.7 copy-done.10
  61.3 8.9 %stencil.4 = (bf16[6,8,64,128]{3,2,1,0:T(8,128)(2,1)}, bf16[8,2,8,128]{3,2,1,0:T(8,128)(2,1)}) custom-call(s32[1]{0:T(128)} %bitcast.refs_0_, f32[2]{0:T(128)} %add_convert_fusion.refs_1_, f32[1,6,8,8,1024]{4,3,2,1,0:T(8,128)} %get-tuple-element.25.refs_2_, bf16[6,4,8,1024]{3,2,1,0:T(8,128)(2,1)} %copy-done.10, bf16[6,4,8,1024]{3,2,1,0:T(8,128)(2,1)} %copy-done.11, ...), custom_call_target="tpu_custom_call" | custom-call | tf_op jit(solution)/shard_map/stencil/pallas_call | solution.py:218
  70.3 0.8 fusion.67
  71.9 4.8 %collective-permute-done.9 = bf16[4,8,2,8,128]{4,3,2,1,0:T(8,128)(2,1)S(1)} collective-permute-done((bf16[4,8,2,8,128]{4,3,2,1,0:T(8,128)(2,1)S(1)}, bf16[4,8,2,8,128]{4,3,2,1,0:T(8,128)(2,1)S(1)}, u32[]{:S(2)}, u32[]{:S(2)}) %collective-permute-start.9) | collective-permute-done | bytes 131104 | tf_op jit(solution)/shard_map/ppermute | solution.py:306
  78.5 2.6 %collective-permute-start.11 = (bf16[8,1,65,128]{2,3,1,0:T(8,128)(2,1)S(1)}, bf16[8,1,65,128]{2,3,1,0:T(8,128)(2,1)S(1)}, u32[]{:S(2)}, u32[]{:S(2)}) collective-permute-start(bf16[8,1,65,128]{2,3,1,0:T(8,128)(2,1)S(1)} %fusion.47), channel_id=1, source_target_pairs={{1,2},{3,4},{5,6},{7,8},{9,10},{11,12},{13,14},{2,1},{4,3},{6,5},{... | collective-permute-start | bytes 399368 | tf_op jit(solution)/shard_map/ppermute | solution.py:319
  81.7 1.5 collective-permute-start.14
  83.7 1.5 collective-permute-start.18
  85.2 2.0 %collective-permute-done.11 = bf16[8,1,65,128]{2,3,1,0:T(8,128)(2,1)S(1)} collective-permute-done((bf16[8,1,65,128]{2,3,1,0:T(8,128)(2,1)S(1)}, bf16[8,1,65,128]{2,3,1,0:T(8,128)(2,1)S(1)}, u32[]{:S(2)}, u32[]{:S(2)}) %collective-permute-start.11) | collective-permute-done | bytes 133152 | tf_op jit(solution)/shard_map/ppermute | solution.py:319
  87.5 0.7 fusion.7
  93.4 1.3 fusion.43
  94.7 1.4 fusion.24
  96.1 1.0 slice.144
  97.2 1.8 %fusion = f32[8,2,64,64]{2,3,0,1:T(8,128)S(1)} fusion(f32[8,2,64,64]{3,2,0,1:T(8,128)} %fusion.43, f32[8,2,64,64]{3,2,1,0:T(8,128)} %fusion.24, f32[64,64]{0,1:T(8,128)S(1)} %get-tuple-element.86), kind=kOutput, calls=%fused_computation.1 | convolution fusion | flops 25296896 | bytes 802816 | tf_op jit(solution)/shard_map/dot_general | solution.py:414
  99.0 2.4 %fusion.22 = f32[8,2,64,64]{2,3,1,0:T(8,128)} fusion(f32[8,2,64,64]{3,2,1,0:T(8,128)} %fusion.24, f32[8,2,64,64]{2,3,0,1:T(8,128)S(1)} %fusion), kind=kOutput, calls=%fused_computation.52 | convolution fusion | flops 25165824 | bytes 786432 | tf_op jit(solution)/shard_map/dot_general | solution.py:416
  101.4 1.2 copy.122
  102.7 1.6 convolution_bitcast_fusion
  104.3 1.6 fusion.72
  106.0 1.2 fusion.69
  107.4 2.6 %collective-permute-start.19 = (f32[12,32]{1,0:T(8,128)S(1)}, f32[12,32]{1,0:T(8,128)S(1)}, u32[]{:S(2)}, u32[]{:S(2)}) collective-permute-start(f32[12,32]{1,0:T(8,128)S(1)} %fusion.59), channel_id=1, source_target_pairs={{0,1},{1,0},{2,3},{3,2},{4,5},{5,4},{6,7},{7,6},{8,9},{9,8},{10,11... | collective-permute-start | bytes 4616 | tf_op jit(solution)/shard_map/ppermute | solution.py:443
  110.0 0.8 collective-permute-done.19
  110.9 1.1 collective-permute-start.20
  112.0 2.5 %collective-permute-done.20 = f32[12,32]{1,0:T(8,128)S(1)} collective-permute-done((f32[12,32]{1,0:T(8,128)S(1)}, f32[12,32]{1,0:T(8,128)S(1)}, u32[]{:S(2)}, u32[]{:S(2)}) %collective-permute-start.20) | collective-permute-done | bytes 1568 | tf_op jit(solution)/shard_map/ppermute | solution.py:443
  114.5 3.6 %collective-permute-done.21 = f32[12,32]{1,0:T(8,128)S(1)} collective-permute-done((f32[12,32]{1,0:T(8,128)S(1)}, f32[12,32]{1,0:T(8,128)S(1)}, u32[]{:S(2)}, u32[]{:S(2)}) %collective-permute-start.21) | collective-permute-done | bytes 1568 | tf_op jit(solution)/shard_map/ppermute | solution.py:443
  118.7 22.0 %collective-permute-done.18.refs_9_ = bf16[2,8,64,128]{3,2,1,0:T(8,128)(2,1)} collective-permute-done((bf16[2,8,64,128]{3,2,1,0:T(8,128)(2,1)}, bf16[2,8,64,128]{3,2,1,0:T(8,128)(2,1)}, u32[]{:S(2)}, u32[]{:S(2)}) %collective-permute-start.18) | collective-permute-done | bytes 262176 | tf_op jit(solution)/shard_map/ppermute | solution.py:306
  140.7 6.5 %collective-permute-start.22 = (f32[12,32]{1,0:T(8,128)S(1)}, f32[12,32]{1,0:T(8,128)S(1)}, u32[]{:S(2)}, u32[]{:S(2)}) collective-permute-start(f32[12,32]{1,0:T(8,128)S(1)} %add.153), channel_id=1, source_target_pairs={{0,8},{1,9},{2,10},{3,11},{4,12},{5,13},{6,14},{7,15},{8,0},{9,1},... | collective-permute-start | bytes 4616 | tf_op jit(solution)/shard_map/ppermute | solution.py:443
  147.2 1.1 add_bitcast_fusion
  148.3 0.9 copy.157
  149.1 2.3 %spread.1 = (bf16[2,256,512]{2,1,0:T(8,128)(2,1)}, bf16[2,256,512]{2,1,0:T(8,128)(2,1)}) custom-call(f32[2,256,64]{2,1,0:T(8,128)} %bitcast.101), custom_call_target="tpu_custom_call" | custom-call | tf_op jit(solution)/shard_map/spread/pallas_call | solution.py:258
  151.7 1.7 %collective-permute-start.15 = (bf16[1,8,64,128]{3,2,1,0:T(8,128)(2,1)}, bf16[1,8,64,128]{3,2,1,0:T(8,128)(2,1)S(1)}, u32[]{:S(2)}, u32[]{:S(2)}) collective-permute-start(bf16[1,8,64,128]{3,2,1,0:T(8,128)(2,1)} %get-tuple-element.44.refs_5_), channel_id=1, source_target_pairs={{16,0},{0,16},{17,1},{1,17},{18,2},{2,18},{19,3},{3,19},{20,4},{4,... | collective-permute-start | bytes 393224 | tf_op jit(solution)/shard_map/ppermute | solution.py:306
  154.1 4.0 %update.4.refs_10_ = bf16[32,6,8,1024]{3,2,1,0:T(8,128)(2,1)} custom-call(bf16[2,256,512]{2,1,0:T(8,128)(2,1)} %get-tuple-element.39.refs_0_, bf16[2,256,512]{2,1,0:T(8,128)(2,1)} %get-tuple-element.40.refs_1_, bf16[6,8,64,128]{3,2,1,0:T(8,128)(2,1)} %get-tuple-element.41.refs_2_, bf16[6,8,64,128]{3,2,1,0:T(8,128)(2,1)} %get-tuple-element.42.refs_3_, ...), custom_call_target="tpu_custom_call" | custom-call | tf_op jit(solution)/shard_map/update/pallas_call | solution.py:293
  158.2 4.1 %update.5.refs_10_ = bf16[32,6,8,1024]{3,2,1,0:T(8,128)(2,1)} custom-call(bf16[2,256,512]{2,1,0:T(8,128)(2,1)} %get-tuple-element.39.refs_0_, bf16[2,256,512]{2,1,0:T(8,128)(2,1)} %get-tuple-element.40.refs_1_, bf16[6,8,64,128]{3,2,1,0:T(8,128)(2,1)} %get-tuple-element.41.refs_2_, ...), custom_call_target="tpu_custom_call", output_to_operand_aliasing={{}: (10, {})} | custom-call | tf_op jit(solution)/shard_map/update/pallas_call | solution.py:293
  162.3 3.0 %update.6.refs_10_ = bf16[32,6,8,1024]{3,2,1,0:T(8,128)(2,1)} custom-call(bf16[2,256,512]{2,1,0:T(8,128)(2,1)} %get-tuple-element.39.refs_0_, bf16[2,256,512]{2,1,0:T(8,128)(2,1)} %get-tuple-element.40.refs_1_, bf16[6,8,64,128]{3,2,1,0:T(8,128)(2,1)} %get-tuple-element.41.refs_2_, ...), custom_call_target="tpu_custom_call", output_to_operand_aliasing={{}: (10, {})} | custom-call | tf_op jit(solution)/shard_map/update/pallas_call | solution.py:293
  165.9 3.0 %update.7 = bf16[32,6,8,1024]{3,2,1,0:T(8,128)(2,1)} custom-call(bf16[2,256,512]{2,1,0:T(8,128)(2,1)} %get-tuple-element.39.refs_0_, bf16[2,256,512]{2,1,0:T(8,128)(2,1)} %get-tuple-element.40.refs_1_, bf16[6,8,64,128]{3,2,1,0:T(8,128)(2,1)} %get-tuple-element.41.refs_2_, ...), custom_call_target="tpu_custom_call", output_to_operand_aliasing={{}: (10, {})} | custom-call | tf_op jit(solution)/shard_map/update/pallas_call | solution.py:293
  (117 shorter events, 14.1 us)
Async XLA Ops:
  0.6 11.3 %copy-start.17 = (s32[8,1,128]{2,1,0:T(1,128)S(1)}, s32[8,1,128]{2,1,0:T(1,128)}, u32[]{:S(2)}) copy-start(s32[8,1,128]{2,1,0:T(1,128)} %param.10) | copy-start | bytes 12292
  0.7 11.3 %copy-start.16 = (f32[32,12]{0,1:T(8,128)S(1)}, f32[32,12]{0,1:T(8,128)}, u32[]{:S(2)}) copy-start(f32[32,12]{0,1:T(8,128)} %param.8) | copy-start | bytes 4612
  0.7 11.3 %copy-start.19 = (f32[8,1,128]{2,1,0:T(1,128)S(1)}, f32[8,1,128]{2,1,0:T(1,128)}, u32[]{:S(2)}) copy-start(f32[8,1,128]{2,1,0:T(1,128)} %param.12) | copy-start | bytes 12292
  0.7 11.3 %copy-start.20 = (f32[8,1,128]{2,1,0:T(1,128)S(1)}, f32[8,1,128]{2,1,0:T(1,128)}, u32[]{:S(2)}) copy-start(f32[8,1,128]{2,1,0:T(1,128)} %param.11) | copy-start | bytes 12292
  0.7 14.7 %copy-start.21 = (s32[8]{0:T(128)S(1)}, s32[8]{0:T(128)}, u32[]{:S(2)}) copy-start(s32[8]{0:T(128)} %param.13) | copy-start | bytes 100
  0.7 14.7 %copy-start.18 = (s32[12,6]{0,1:T(8,128)S(1)}, s32[12,6]{0,1:T(8,128)}, u32[]{:S(2)}) copy-start(s32[12,6]{0,1:T(8,128)} %param.9) | copy-start | bytes 868
  8.4 12.4 %collective-permute-start.3 = (bf16[6,4,8,1024]{3,2,1,0:T(8,128)(2,1)}, bf16[6,4,8,1024]{3,2,1,0:T(8,128)(2,1)S(1)}, u32[]{:S(2)}, u32[]{:S(2)}) collective-permute-start(bf16[6,4,8,1024]{3,2,1,0:T(8,128)(2,1)} %get-tuple-element.30), channel_id=1, source_target_pairs={{0,1},{1,0},{2,3},{3,2},{4,5},{5,4},{6,7},{7,6},{8,9},{9,8},{10,11... | collective-permute-start | bytes 1179656 | tf_op jit(solution)/shard_map/ppermute | solution.py:314
  8.5 15.5 %collective-permute-start.4 = (bf16[6,4,8,1024]{3,2,1,0:T(8,128)(2,1)}, bf16[6,4,8,1024]{3,2,1,0:T(8,128)(2,1)S(1)}, u32[]{:S(2)}, u32[]{:S(2)}) collective-permute-start(bf16[6,4,8,1024]{3,2,1,0:T(8,128)(2,1)} %get-tuple-element.31), channel_id=1, source_target_pairs={{1,2},{3,4},{5,6},{7,8},{9,10},{11,12},{13,14},{2,1},{4,3},{6,5},{... | collective-permute-start | bytes 1179656 | tf_op jit(solution)/shard_map/ppermute | solution.py:319
  12.0 8.2 %collective-permute-start.2 = (f32[40,128]{1,0:T(8,128)S(1)}, f32[40,128]{1,0:T(8,128)S(1)}, u32[]{:S(2)}, u32[]{:S(2)}) collective-permute-start(f32[40,128]{1,0:T(8,128)S(1)} %get-tuple-element.70), channel_id=1, source_target_pairs={{16,0},{0,16},{17,1},{1,17},{18,2},{2,18},{19,3},{3,19},{20,4},{4,... | collective-permute-start | bytes 61448 | tf_op jit(solution)/shard_map/ppermute | solution.py:306
  12.6 14.4 %collective-permute-start.5 = (bf16[6,4,8,1024]{3,2,1,0:T(8,128)(2,1)}, bf16[6,4,8,1024]{3,2,1,0:T(8,128)(2,1)S(1)}, u32[]{:S(2)}, u32[]{:S(2)}) collective-permute-start(bf16[6,4,8,1024]{3,2,1,0:T(8,128)(2,1)} %get-tuple-element.33), channel_id=1, source_target_pairs={{0,1},{1,0},{2,3},{3,2},{4,5},{5,4},{6,7},{7,6},{8,9},{9,8},{10,11... | collective-permute-start | bytes 1179656 | tf_op jit(solution)/shard_map/ppermute | solution.py:314
  12.6 27.5 %collective-permute-start.6 = (bf16[6,4,8,1024]{3,2,1,0:T(8,128)(2,1)}, bf16[6,4,8,1024]{3,2,1,0:T(8,128)(2,1)S(1)}, u32[]{:S(2)}, u32[]{:S(2)}) collective-permute-start(bf16[6,4,8,1024]{3,2,1,0:T(8,128)(2,1)} %get-tuple-element.34), channel_id=1, source_target_pairs={{1,2},{3,4},{5,6},{7,8},{9,10},{11,12},{13,14},{2,1},{4,3},{6,5},{... | collective-permute-start | bytes 1179656 | tf_op jit(solution)/shard_map/ppermute | solution.py:319
  20.2 40.2 %collective-permute-start = (bf16[6,4,8,1024]{3,2,1,0:T(8,128)(2,1)}, bf16[6,4,8,1024]{3,2,1,0:T(8,128)(2,1)S(1)}, u32[]{:S(2)}, u32[]{:S(2)}) collective-permute-start(bf16[6,4,8,1024]{3,2,1,0:T(8,128)(2,1)} %get-tuple-element.26), channel_id=1, source_target_pairs={{0,1},{1,0},{2,3},{3,2},{4,5},{5,4},{6,7},{7,6},{8,9},{9,8},{10,11... | collective-permute-start | bytes 1179656 | tf_op jit(solution)/shard_map/ppermute | solution.py:314
  20.9 10.2 %copy-start.4 = (bf16[6,4,8,1024]{3,2,1,0:T(8,128)(2,1)}, bf16[6,4,8,1024]{3,2,1,0:T(8,128)(2,1)S(1)}, u32[]{:S(2)}) copy-start(bf16[6,4,8,1024]{3,2,1,0:T(8,128)(2,1)S(1)} %collective-permute-done.3.refs_3_) | copy-start | bytes 1179652
  20.9 39.6 %collective-permute-start.1 = (bf16[6,4,8,1024]{3,2,1,0:T(8,128)(2,1)}, bf16[6,4,8,1024]{3,2,1,0:T(8,128)(2,1)S(1)}, u32[]{:S(2)}, u32[]{:S(2)}) collective-permute-start(bf16[6,4,8,1024]{3,2,1,0:T(8,128)(2,1)} %get-tuple-element.27), channel_id=1, source_target_pairs={{1,2},{3,4},{5,6},{7,8},{9,10},{11,12},{13,14},{2,1},{4,3},{6,5},{... | collective-permute-start | bytes 1179656 | tf_op jit(solution)/shard_map/ppermute | solution.py:319
  24.0 7.1 %copy-start.5 = (bf16[6,4,8,1024]{3,2,1,0:T(8,128)(2,1)}, bf16[6,4,8,1024]{3,2,1,0:T(8,128)(2,1)S(1)}, u32[]{:S(2)}) copy-start(bf16[6,4,8,1024]{3,2,1,0:T(8,128)(2,1)S(1)} %collective-permute-done.4.refs_4_) | copy-start | bytes 1179652
  24.0 25.8 %collective-permute-start.7 = (bf16[6,4,8,1024]{3,2,1,0:T(8,128)(2,1)}, bf16[6,4,8,1024]{3,2,1,0:T(8,128)(2,1)S(1)}, u32[]{:S(2)}, u32[]{:S(2)}) collective-permute-start(bf16[6,4,8,1024]{3,2,1,0:T(8,128)(2,1)} %get-tuple-element.36), channel_id=1, source_target_pairs={{0,1},{1,0},{2,3},{3,2},{4,5},{5,4},{6,7},{7,6},{8,9},{9,8},{10,11... | collective-permute-start | bytes 1179656 | tf_op jit(solution)/shard_map/ppermute | solution.py:314
  27.0 13.0 %copy-start.6 = (bf16[6,4,8,1024]{3,2,1,0:T(8,128)(2,1)}, bf16[6,4,8,1024]{3,2,1,0:T(8,128)(2,1)S(1)}, u32[]{:S(2)}) copy-start(bf16[6,4,8,1024]{3,2,1,0:T(8,128)(2,1)S(1)} %collective-permute-done.5.refs_3_) | copy-start | bytes 1179652
  27.1 22.8 %collective-permute-start.8 = (bf16[6,4,8,1024]{3,2,1,0:T(8,128)(2,1)}, bf16[6,4,8,1024]{3,2,1,0:T(8,128)(2,1)S(1)}, u32[]{:S(2)}, u32[]{:S(2)}) collective-permute-start(bf16[6,4,8,1024]{3,2,1,0:T(8,128)(2,1)} %get-tuple-element.37), channel_id=1, source_target_pairs={{1,2},{3,4},{5,6},{7,8},{9,10},{11,12},{13,14},{2,1},{4,3},{6,5},{... | collective-permute-start | bytes 1179656 | tf_op jit(solution)/shard_map/ppermute | solution.py:319
  40.1 0.8 copy-start.7
  49.8 20.5 %copy-start.14 = (bf16[8,2,8,128]{3,2,1,0:T(8,128)(2,1)S(1)}, bf16[8,2,8,128]{3,2,1,0:T(8,128)(2,1)}, u32[]{:S(2)}) copy-start(bf16[8,2,8,128]{3,2,1,0:T(8,128)(2,1)} %get-tuple-element.32) | copy-start | bytes 98308
  49.8 20.5 %copy-start.15 = (bf16[8,2,8,128]{3,2,1,0:T(8,128)(2,1)S(1)}, bf16[8,2,8,128]{3,2,1,0:T(8,128)(2,1)}, u32[]{:S(2)}) copy-start(bf16[8,2,8,128]{3,2,1,0:T(8,128)(2,1)} %get-tuple-element.35) | copy-start | bytes 98308
  49.9 0.8 copy-start.8
  50.6 0.8 copy-start.9
  60.4 0.8 copy-start.10
  60.5 0.9 copy-start.11
  71.1 5.6 %collective-permute-start.9 = (bf16[4,8,2,8,128]{4,3,2,1,0:T(8,128)(2,1)S(1)}, bf16[4,8,2,8,128]{4,3,2,1,0:T(8,128)(2,1)S(1)}, u32[]{:S(2)}, u32[]{:S(2)}) collective-permute-start(bf16[4,8,2,8,128]{4,3,2,1,0:T(8,128)(2,1)S(1)} %get-tuple-element.65), channel_id=1, source_target_pairs={{16,0},{0,16},{17,1},{1,17},{18,2},{2,18},{19,3},{3,19},{20,4},{4,... | collective-permute-start | bytes 393224 | tf_op jit(solution)/shard_map/ppermute | solution.py:306
  76.9 4.1 %copy-start = (bf16[6,8,64,128]{3,2,1,0:T(8,128)(2,1)S(1)}, bf16[6,8,64,128]{3,2,1,0:T(8,128)(2,1)}, u32[]{:S(2)}) copy-start(bf16[6,8,64,128]{3,2,1,0:T(8,128)(2,1)} %get-tuple-element.42.refs_3_) | copy-start | bytes 2359300
  76.9 4.7 %copy-start.1 = (bf16[6,8,64,128]{3,2,1,0:T(8,128)(2,1)S(1)}, bf16[6,8,64,128]{3,2,1,0:T(8,128)(2,1)}, u32[]{:S(2)}) copy-start(bf16[6,8,64,128]{3,2,1,0:T(8,128)(2,1)} %get-tuple-element.43.refs_4_) | copy-start | bytes 2359300
  76.9 6.2 %copy-start.2 = (bf16[6,8,64,128]{3,2,1,0:T(8,128)(2,1)S(1)}, bf16[6,8,64,128]{3,2,1,0:T(8,128)(2,1)}, u32[]{:S(2)}) copy-start(bf16[6,8,64,128]{3,2,1,0:T(8,128)(2,1)} %get-tuple-element.41.refs_2_) | copy-start | bytes 2359300
  78.4 5.3 %collective-permute-start.10 = (bf16[8,1,65,128]{2,3,1,0:T(8,128)(2,1)S(1)}, bf16[8,1,65,128]{2,3,1,0:T(8,128)(2,1)S(1)}, u32[]{:S(2)}, u32[]{:S(2)}) collective-permute-start(bf16[8,1,65,128]{2,3,1,0:T(8,128)(2,1)S(1)} %fusion.47), channel_id=1, source_target_pairs={{0,1},{1,0},{2,3},{3,2},{4,5},{5,4},{6,7},{7,6},{8,9},{9,8},{10,11... | collective-permute-start | bytes 399368 | tf_op jit(solution)/shard_map/ppermute | solution.py:314
  78.5 8.7 %collective-permute-start.11 = (bf16[8,1,65,128]{2,3,1,0:T(8,128)(2,1)S(1)}, bf16[8,1,65,128]{2,3,1,0:T(8,128)(2,1)S(1)}, u32[]{:S(2)}, u32[]{:S(2)}) collective-permute-start(bf16[8,1,65,128]{2,3,1,0:T(8,128)(2,1)S(1)} %fusion.47), channel_id=1, source_target_pairs={{1,2},{3,4},{5,6},{7,8},{9,10},{11,12},{13,14},{2,1},{4,3},{6,5},{... | collective-permute-start | bytes 399368 | tf_op jit(solution)/shard_map/ppermute | solution.py:319
  81.1 70.7 %collective-permute-start.13 = (bf16[6,8,64,128]{3,2,1,0:T(8,128)(2,1)S(1)}, bf16[6,8,64,128]{3,2,1,0:T(8,128)(2,1)S(1)}, u32[]{:S(2)}, u32[]{:S(2)}) collective-permute-start(bf16[6,8,64,128]{3,2,1,0:T(8,128)(2,1)S(1)} %copy-done), channel_id=1, source_target_pairs={{16,0},{0,16},{17,1},{1,17},{18,2},{2,18},{19,3},{3,19},{20,4},{4,... | collective-permute-start | bytes 2359304 | tf_op jit(solution)/shard_map/ppermute | solution.py:306
  81.7 72.5 %collective-permute-start.14 = (bf16[6,8,64,128]{3,2,1,0:T(8,128)(2,1)S(1)}, bf16[6,8,64,128]{3,2,1,0:T(8,128)(2,1)}, u32[]{:S(2)}, u32[]{:S(2)}) collective-permute-start(bf16[6,8,64,128]{3,2,1,0:T(8,128)(2,1)S(1)} %copy-done.1), channel_id=1, source_target_pairs={{16,0},{0,16},{17,1},{1,17},{18,2},{2,18},{19,3},{3,19},{20,4},{4,... | collective-permute-start | bytes 2359304 | tf_op jit(solution)/shard_map/ppermute | solution.py:306
  83.1 71.0 %collective-permute-start.12 = (bf16[6,8,64,128]{3,2,1,0:T(8,128)(2,1)S(1)}, bf16[6,8,64,128]{3,2,1,0:T(8,128)(2,1)}, u32[]{:S(2)}, u32[]{:S(2)}) collective-permute-start(bf16[6,8,64,128]{3,2,1,0:T(8,128)(2,1)S(1)} %copy-done.2), channel_id=1, source_target_pairs={{16,0},{0,16},{17,1},{1,17},{18,2},{2,18},{19,3},{3,19},{20,4},{4,... | collective-permute-start | bytes 2359304 | tf_op jit(solution)/shard_map/ppermute | solution.py:306
  83.7 57.0 %collective-permute-start.18 = (bf16[2,8,64,128]{3,2,1,0:T(8,128)(2,1)}, bf16[2,8,64,128]{3,2,1,0:T(8,128)(2,1)}, u32[]{:S(2)}, u32[]{:S(2)}) collective-permute-start(bf16[2,8,64,128]{3,2,1,0:T(8,128)(2,1)} %get-tuple-element.47.refs_5_), channel_id=1, source_target_pairs={{16,0},{0,16},{17,1},{1,17},{18,2},{2,18},{19,3},{3,19},{20,4},{4,... | collective-permute-start | bytes 786440 | tf_op jit(solution)/shard_map/ppermute | solution.py:306
  96.1 22.1 %copy-start.12 = (bf16[2,8,64,128]{3,2,1,0:T(8,128)(2,1)S(1)}, bf16[2,8,64,128]{3,2,1,0:T(8,128)(2,1)}, u32[]{:S(2)}) copy-start(bf16[2,8,64,128]{3,2,1,0:T(8,128)(2,1)} %get-tuple-element.46.refs_5_) | copy-start | bytes 786436
  107.4 3.4 %collective-permute-start.19 = (f32[12,32]{1,0:T(8,128)S(1)}, f32[12,32]{1,0:T(8,128)S(1)}, u32[]{:S(2)}, u32[]{:S(2)}) collective-permute-start(f32[12,32]{1,0:T(8,128)S(1)} %fusion.59), channel_id=1, source_target_pairs={{0,1},{1,0},{2,3},{3,2},{4,5},{5,4},{6,7},{7,6},{8,9},{9,8},{10,11... | collective-permute-start | bytes 4616 | tf_op jit(solution)/shard_map/ppermute | solution.py:443
  110.9 3.7 %collective-permute-start.20 = (f32[12,32]{1,0:T(8,128)S(1)}, f32[12,32]{1,0:T(8,128)S(1)}, u32[]{:S(2)}, u32[]{:S(2)}) collective-permute-start(f32[12,32]{1,0:T(8,128)S(1)} %add.151), channel_id=1, source_target_pairs={{0,2},{1,3},{2,0},{3,1},{4,6},{5,7},{6,4},{7,5},{8,10},{9,11},{10,... | collective-permute-start | bytes 4616 | tf_op jit(solution)/shard_map/ppermute | solution.py:443
  114.5 3.7 %collective-permute-start.21 = (f32[12,32]{1,0:T(8,128)S(1)}, f32[12,32]{1,0:T(8,128)S(1)}, u32[]{:S(2)}, u32[]{:S(2)}) collective-permute-start(f32[12,32]{1,0:T(8,128)S(1)} %add.152), channel_id=1, source_target_pairs={{0,4},{1,5},{2,6},{3,7},{4,0},{5,1},{6,2},{7,3},{8,12},{9,13},{10,... | collective-permute-start | bytes 4616 | tf_op jit(solution)/shard_map/ppermute | solution.py:443
  118.2 40.0 %collective-permute-start.17 = (bf16[2,8,64,128]{3,2,1,0:T(8,128)(2,1)S(1)}, bf16[2,8,64,128]{3,2,1,0:T(8,128)(2,1)}, u32[]{:S(2)}, u32[]{:S(2)}) collective-permute-start(bf16[2,8,64,128]{3,2,1,0:T(8,128)(2,1)S(1)} %copy-done.12), channel_id=1, source_target_pairs={{16,0},{0,16},{17,1},{1,17},{18,2},{2,18},{19,3},{3,19},{20,4},{4,... | collective-permute-start | bytes 786440 | tf_op jit(solution)/shard_map/ppermute | solution.py:306
  140.7 10.7 %collective-permute-start.22 = (f32[12,32]{1,0:T(8,128)S(1)}, f32[12,32]{1,0:T(8,128)S(1)}, u32[]{:S(2)}, u32[]{:S(2)}) collective-permute-start(f32[12,32]{1,0:T(8,128)S(1)} %add.153), channel_id=1, source_target_pairs={{0,8},{1,9},{2,10},{3,11},{4,12},{5,13},{6,14},{7,15},{8,0},{9,1},... | collective-permute-start | bytes 4616 | tf_op jit(solution)/shard_map/ppermute | solution.py:443
  151.4 10.8 %collective-permute-start.16 = (bf16[1,8,64,128]{3,2,1,0:T(8,128)(2,1)}, bf16[1,8,64,128]{3,2,1,0:T(8,128)(2,1)}, u32[]{:S(2)}, u32[]{:S(2)}) collective-permute-start(bf16[1,8,64,128]{3,2,1,0:T(8,128)(2,1)} %get-tuple-element.45.refs_5_), channel_id=1, source_target_pairs={{16,0},{0,16},{17,1},{1,17},{18,2},{2,18},{19,3},{3,19},{20,4},{4,... | collective-permute-start | bytes 393224 | tf_op jit(solution)/shard_map/ppermute | solution.py:306
  151.7 2.4 %copy-start.3 = (bf16[6,8,64,128]{3,2,1,0:T(8,128)(2,1)}, bf16[6,8,64,128]{3,2,1,0:T(8,128)(2,1)S(1)}, u32[]{:S(2)}) copy-start(bf16[6,8,64,128]{3,2,1,0:T(8,128)(2,1)S(1)} %collective-permute-done.13.refs_7_) | copy-start | bytes 2359300
  151.7 13.6 %collective-permute-start.15 = (bf16[1,8,64,128]{3,2,1,0:T(8,128)(2,1)}, bf16[1,8,64,128]{3,2,1,0:T(8,128)(2,1)S(1)}, u32[]{:S(2)}, u32[]{:S(2)}) collective-permute-start(bf16[1,8,64,128]{3,2,1,0:T(8,128)(2,1)} %get-tuple-element.44.refs_5_), channel_id=1, source_target_pairs={{16,0},{0,16},{17,1},{1,17},{18,2},{2,18},{19,3},{3,19},{20,4},{4,... | collective-permute-start | bytes 393224 | tf_op jit(solution)/shard_map/ppermute | solution.py:306
  165.3 0.7 copy-start.13

commit v2 on v1

v2 whole, which is shorter than its diff:
```python
import math

import jax
import jax.numpy as jnp
from jax import lax
from jax.experimental import pallas as pl
from jax.experimental.pallas import tpu as pltpu
from jax.sharding import PartitionSpec as P


HALO = 8
STEPS = 4
NS_STEPS = 5
LANES = 128
TILE = 8
PACE = 4
KERNEL_VMEM = 44 * 1024 * 1024
ODD, ME, OPEN = 0, 1, 2

diffusion = 0.2
advection = 0.15
vertical = 0.1
coupling = 0.2


def planes_of(fields, levels):
    return [(f, l) for f in range(fields) for l in range(levels)]


def pack_kernel(fields, rows, levels, cols, count, flags_ref, x_ref, *rest):
    outs, turned, edges, sems = rest[:2 * count + 1], *rest[2 * count + 1:]
    groups = cols // LANES
    stride = fields * rows * levels * groups
    planes = fields * levels
    tile = pl.program_id(0)

    def row(y, _):
        for p, (f, l) in enumerate(planes_of(fields, levels)):
            for s in range(groups):
                start = ((f * rows + y) * levels + l) * groups + s
                turned[tile, p, y, :, s * LANES:(s + 1) * LANES] = x_ref[pl.ds(start, TILE, stride=stride), :]
        return 0

    lax.fori_loop(0, rows, row, 0)

    def edge(y, _):
        for side in range(2):
            at = jnp.where(flags_ref[ODD] == side, rows - STEPS, 0) + y
            for p in range(planes):
                edges[tile, side, p, y] = turned[tile, p, at].astype(jnp.bfloat16)
        return 0

    lax.fori_loop(0, STEPS, edge, 0)

    def copies(k):
        pairs = [(edges.at[k, 0], outs[2 * k]), (edges.at[k, 1], outs[2 * k + 1]), (turned.at[k], outs[-1].at[k])]
        return [pltpu.make_async_copy(src, dst, sems.at[k, i]) for i, (src, dst) in enumerate(pairs)]

    for k in range(count):
        @pl.when(tile == k)
        def _():
            for copy in copies(k):
                copy.start()

    @pl.when(tile == count - 1)
    def _():
        for k in range(count):
            for copy in copies(k):
                copy.wait()


def pack(flags, x2, first, count, fields, rows, levels, cols):
    planes = fields * levels
    block = TILE * fields * rows * levels * cols // LANES
    edge = (planes, STEPS, TILE, cols)
    turned = (count, planes, rows, TILE, cols)
    return pl.pallas_call(
        lambda *refs: pack_kernel(fields, rows, levels, cols, count, *refs),
        grid=(count,),
        in_specs=[pl.BlockSpec(memory_space=pltpu.SMEM), pl.BlockSpec((block, LANES), lambda i: (first + i, 0))],
        out_specs=[pl.BlockSpec(memory_space=pltpu.HBM)] * (2 * count + 1),
        out_shape=[jax.ShapeDtypeStruct(edge, jnp.bfloat16)] * (2 * count) + [jax.ShapeDtypeStruct(turned, jnp.float32)],
        scratch_shapes=[
            pltpu.VMEM(turned, jnp.float32),
            pltpu.VMEM((count, 2, *edge), jnp.bfloat16),
            pltpu.SemaphoreType.DMA((count, 3)),
        ],
        name="pack",
    )(flags, pltpu.with_memory_space_constraint(x2, pltpu.HBM))


def stencil_kernel(fields, rows, levels, cols, blocks, splits, local, held, flags_ref, x_ref, first_ref, second_ref, coef_ref, *rest):
    small_refs, rest = rest[:blocks], rest[blocks + held:]
    out_refs = rest[:len(splits)]
    obs_ref = rest[len(splits)]
    *state, mixed, sem = rest[len(splits) + 1:]
    groups = cols // LANES
    block_cols = cols // blocks
    pairs = planes_of(fields, levels)
    planes = len(pairs)

    own_copy = pltpu.make_async_copy(x_ref.at[local], state[0].at[:, pl.ds(STEPS, rows)], sem)
    own_copy.start()

    def tile_at(s):
        return slice(s * LANES, (s + 1) * LANES)

    odd = flags_ref[ODD] == 1

    def load_edge(y, _):
        for p in range(planes):
            first = first_ref[p, y].astype(jnp.float32)
            second = second_ref[p, y].astype(jnp.float32)
            state[0][p, y] = jnp.where(odd, first, second)
            state[0][p, STEPS + rows + y] = jnp.where(odd, second, first)
        return 0

    lax.fori_loop(0, STEPS, load_edge, 0)
    own_copy.wait()
    is_open = [flags_ref[OPEN + side].astype(jnp.float32) for side in range(2)]

    lane = lax.broadcasted_iota(jnp.int32, (TILE, LANES), 1)
    at_last = lane == LANES - 1
    at_first = lane == 0
    centre = (1.0 - 4.0 * diffusion - vertical) / diffusion
    below_part = vertical / diffusion
    right_part = (diffusion - advection) / diffusion
    left_part = (diffusion + advection) / diffusion
    next_part = coupling / diffusion
    scale = diffusion ** STEPS
    coefs = [jnp.broadcast_to(next_part * coef_ref[:, f:f + 1], (TILE, LANES)) for f in range(fields)]

    def rest_of_step(src, y, p):
        f, l = pairs[p]
        after = ((f + 1) % fields) * levels + l
        under = f * levels + (l - 1) % levels
        mid, out = [], []
        for s in range(groups):
            here = src[p, y, :, tile_at(s)]
            around = src[p, y + 1, :, tile_at(s)] + src[p, y - 1, :, tile_at(s)]
            if under == p:
                whole = centre + below_part
                own = here if abs(whole - 1.0) < 1e-12 else whole * here
            else:
                own = centre * here + below_part * src[under, y, :, tile_at(s)]
            mid.append(here)
            out.append((around + own) + coefs[f] * src[after, y, :, tile_at(s)])
        return mid, out

    def shifted(tiles):
        moved = []
        for s in range(0, groups, 2):
            both = jnp.concatenate(tiles[s:s + 2], axis=0).astype(jnp.bfloat16)
            both = pltpu.roll(both, LANES - 1, 1).astype(jnp.float32)
            moved += [both[k:k + TILE] for k in range(0, both.shape[0], TILE)]
        return moved

    pace = PACE if rows % PACE == 0 else 1
    for t in range(1, STEPS + 1):
        src, dst = state[(t - 1) % 2], state[t % 2]
        reach = STEPS - t
        ratio = math.comb(STEPS, t - 1) / math.comb(STEPS, t)

        def edge_rows(i, _):
            for side, y in enumerate((t + i, STEPS + rows + i)):
                for p in range(planes):
                    for s, value in enumerate(rest_of_step(src, y, p)[1]):
                        dst[p, y, :, tile_at(s)] = value * is_open[side]
            return 0

        def own_rows(i, _):
            for k in range(pace):
                mine = pace * i + k
                for p in range(planes):
                    mid, out = rest_of_step(src, STEPS + mine, p)
                    if t > 1:
                        mid = [mixed[p, mine, :, tile_at(s)] for s in range(groups)]
                    ahead = shifted(mid)
                    behind = [pltpu.roll(v, 1, 1) for v in mid]
                    for s in range(groups):
                        right = jnp.where(at_last, ahead[(s + 1) % groups], ahead[s])
                        left = jnp.where(at_first, behind[(s - 1) % groups], behind[s])
                        value = out[s] + (ratio * right_part * right + ratio * left_part * left)
                        if t < STEPS:
                            dst[p, STEPS + mine, :, tile_at(s)] = out[s]
                            mixed[p, mine, :, tile_at(s)] = value
                            continue
                        value = value * scale
                        mixed[p, mine, :, tile_at(s)] = value
                        for g, (start, count) in enumerate(splits):
                            if start <= p < start + count:
                                at = pl.ds(pl.multiple_of(mine * TILE, TILE), TILE)
                                out_refs[g][p - start, s, at, :] = value.astype(jnp.bfloat16)
            return 0

        if reach:
            lax.fori_loop(0, reach, edge_rows, 0)
        lax.fori_loop(0, rows // pace, own_rows, 0)

    column = lax.broadcasted_iota(jnp.int32, (block_cols, LANES), 0)

    def observe(i, _):
        for k in range(pace):
            y = pace * i + k
            for b in range(blocks):
                cell = small_refs[b][pl.ds(y, 1), :].astype(jnp.int32)
                plane = cell // block_cols
                pick = jnp.where(column == cell - plane * block_cols, 1.0, 0.0).astype(jnp.bfloat16)
                start = (flags_ref[ME] + b) % blocks * block_cols
                part = mixed[:, y, :, pl.ds(pl.multiple_of(start, LANES), block_cols)]
                part = part.reshape(planes * TILE, block_cols).astype(jnp.bfloat16)
                found = jnp.dot(part, pick, preferred_element_type=jnp.float32).reshape(planes, TILE, LANES)
                total = jnp.zeros((TILE, LANES), jnp.float32)
                for p in range(planes):
                    total = jnp.where(plane == p, found[p], total)
                obs_ref[0, y, b] = total.astype(jnp.bfloat16)
        return 0

    lax.fori_loop(0, rows // pace, observe, 0)


def stencil(flags, turned, first, second, coef, smalls, held, tile, local, splits, fields, rows, levels, cols):
    planes = fields * levels
    blocks = len(smalls)
    tiles = coef.shape[0] // TILE
    outs = [jax.ShapeDtypeStruct((count, cols // LANES, rows * TILE, LANES), jnp.bfloat16) for _, count in splits]
    observed = jax.ShapeDtypeStruct((tiles, rows, blocks, TILE, LANES), jnp.bfloat16)
    room = pltpu.VMEM((planes, rows + 2 * STEPS, TILE, cols), jnp.float32)
    far = pl.BlockSpec(memory_space=pltpu.HBM)

    near = pl.BlockSpec(memory_space=pltpu.VMEM)
    in_specs = [pl.BlockSpec(memory_space=pltpu.SMEM), far, near, near, pl.BlockSpec((TILE, fields), lambda i: (tile, 0))]
    in_specs += [near] * len(smalls)
    args = [flags, pltpu.with_memory_space_constraint(turned, pltpu.HBM), first, second, coef, *(near_core(small) for small in smalls)]
    aliases = {}
    if held is not None:
        aliases = {len(args): len(splits)}
        in_specs.append(far)
        args.append(held)
    return pl.pallas_call(
        lambda *refs: stencil_kernel(fields, rows, levels, cols, blocks, splits, local, len(aliases), *refs),
        grid=(1,),
        in_specs=in_specs,
        out_specs=[pl.BlockSpec(out.shape, lambda i: (0, 0, 0, 0)) for out in outs]
        + [pl.BlockSpec((1, *observed.shape[1:]), lambda i: (tile, 0, 0, 0, 0))],
        out_shape=[*outs, observed],
        scratch_shapes=[
            room,
            room,
            pltpu.VMEM((planes, rows, TILE, cols), jnp.float32),
            pltpu.SemaphoreType.DMA,
        ],
        input_output_aliases=aliases,
        compiler_params=pltpu.CompilerParams(vmem_limit_bytes=KERNEL_VMEM),
        name="stencil",
    )(*args)


def product(a, b):
    a_high = a.astype(jnp.bfloat16)
    a_low = (a - a_high.astype(jnp.float32)).astype(jnp.bfloat16)
    b_high = b.astype(jnp.bfloat16)
    b_low = (b - b_high.astype(jnp.float32)).astype(jnp.bfloat16)
    left = jnp.concatenate([a_high, a_low], axis=1)
    right = jnp.concatenate(
        [jnp.concatenate([b_high, b_low], axis=1), jnp.concatenate([b_high, jnp.zeros_like(b_low)], axis=1)], axis=0
    )
    both = jnp.dot(left, right, preferred_element_type=jnp.float32)
    return both[:, :b.shape[1]] + both[:, b.shape[1]:]


def solve_kernel(rows, members, ensemble, pairs, flags_ref, table_ref, own_ref, near_ref, far_ref, upper_ref, lower_ref, sum_ref, wide, ys, zs, ms, gs, scales, direct):
    width = 2 * ensemble
    count = rows * pairs
    odd = flags_ref[ODD] == 1

    def fill(r, _):
        for q in range(pairs):
            near = near_ref[r, q].astype(jnp.float32)
            far = far_ref[r, q].astype(jnp.float32)
            wide[r, q] = jnp.where(odd, near, far)
            wide[rows + r, q] = own_ref[r, q]
            wide[2 * rows + r, q] = jnp.where(odd, far, near)
        return 0

    lax.fori_loop(0, rows, fill, 0)

    lane = lax.broadcasted_iota(jnp.int32, (ensemble, width), 1)
    first = lane < ensemble
    eye = jnp.where(
        lax.broadcasted_iota(jnp.int32, (width, width), 0) == lax.broadcasted_iota(jnp.int32, (width, width), 1), 1.0, 0.0
    )
    first_row = lax.broadcasted_iota(jnp.int32, (TILE, width), 1) < ensemble

    def localize(y, _):
        for q in range(pairs):
            local = jnp.zeros(wide.shape[2:], jnp.float32)
            for d in range(-HALO, HALO + 1):
                local = local + table_ref[d + HALO, y] * wide[rows + y + d, q]
            gram = local[:ensemble]
            amat = jnp.concatenate([jnp.where(first, gram, 0.0), jnp.where(first, 0.0, gram)], axis=0) + (ensemble - 1.0) * eye
            square = amat * amat
            tops = jnp.sqrt(jnp.sum(square[:ensemble], axis=(0, 1), keepdims=True))
            ends = jnp.sqrt(jnp.sum(square[ensemble:], axis=(0, 1), keepdims=True))
            part = jnp.concatenate(
                [jnp.broadcast_to(1.0 / tops, (ensemble, width)), jnp.broadcast_to(1.0 / ends, (ensemble, width))], axis=0
            )
            at = y * pairs + q
            ys[at] = amat * part
            gs[at] = local[ensemble:ensemble + TILE]
            scales[at] = jnp.where(first_row, tops, ends)
        return 0

    lax.fori_loop(0, rows, localize, 0)

    pace = 4 if count % 4 == 0 else 1

    def each(work):
        def some(i, _):
            for k in range(pace):
                work(pace * i + k)
            return 0

        lax.fori_loop(0, count // pace, some, 0)

    for step_idx in range(NS_STEPS):
        def middle(i):
            ms[i] = 1.5 * eye - 0.5 * (product(zs[i], ys[i]) if step_idx else ys[i])

        def apply(i):
            if step_idx < NS_STEPS - 1:
                ys[i] = product(ys[i], ms[i])
            zs[i] = product(ms[i], zs[i]) if step_idx else ms[i]

        each(middle)
        each(apply)

    def weigh(y, total):
        for q in range(pairs):
            at = y * pairs + q
            z, scale = zs[at], scales[at]
            mean = (product(product(gs[at], z), z) / scale)[:1]
            wpert = z[:members] + z[ensemble:ensemble + members]
            weights = wpert * (math.sqrt(ensemble - 1.0) / jnp.sqrt(scale))[:1] + mean
            total = total + weights
            here = first[:members]
            low = jnp.sum(jnp.where(here, weights, 0.0), axis=1, keepdims=True)
            high = jnp.sum(jnp.where(here, 0.0, weights), axis=1, keepdims=True)
            direct[q, pl.ds(y, members, stride=rows), :] = weights + (1.0 - jnp.where(here, low, high)) / ensemble
        return total

    sum_ref[...] = lax.fori_loop(0, rows, weigh, jnp.zeros((members, width), jnp.float32))

    depth = ensemble * rows
    column = lax.broadcasted_iota(jnp.int32, (width, depth), 1)
    member = column // (rows * TILE) * TILE + column % TILE
    entry = lax.broadcasted_iota(jnp.int32, (width, depth), 0)
    mine = lax.broadcasted_iota(jnp.int32, (members * rows, depth), 0) % rows
    theirs = lax.broadcasted_iota(jnp.int32, (members * rows, depth), 1) // TILE % rows
    keep = mine == theirs
    for half in range(2):
        place = jnp.where(entry == member + half * ensemble, 1.0, 0.0).astype(jnp.bfloat16)
        for q in range(pairs):
            w = direct[q]
            high = w.astype(jnp.bfloat16)
            low = (w - high.astype(jnp.float32)).astype(jnp.bfloat16)
            for part, ref in ((high, upper_ref), (low, lower_ref)):
                spread = jnp.dot(part, place, preferred_element_type=jnp.float32)
                ref[2 * q + half] = jnp.where(keep, spread, 0.0).astype(jnp.bfloat16)


def solve(flags, table, own, near, far, members, ensemble):
    rows, pairs, tall, width = own.shape
    count = rows * pairs
    out = pltpu.VMEM((2 * pairs, members * rows, ensemble * rows), jnp.bfloat16)
    square = pltpu.VMEM((count, width, width), jnp.float32)
    line = pltpu.VMEM((count, TILE, width), jnp.float32)
    smem = pl.BlockSpec(memory_space=pltpu.SMEM)
    vmem = pl.BlockSpec(memory_space=pltpu.VMEM)
    return pl.pallas_call(
        lambda *refs: solve_kernel(rows, members, ensemble, pairs, *refs),
        in_specs=[smem, smem, vmem, vmem, vmem],
        out_specs=[vmem] * 3,
        out_shape=[out, out, jax.ShapeDtypeStruct((members, width), jnp.float32)],
        scratch_shapes=[
            pltpu.VMEM((3 * rows, pairs, tall, width), jnp.float32),
            square, square, square, line, line,
            pltpu.VMEM((pairs, members * rows, width), jnp.float32),
        ],
        compiler_params=pltpu.CompilerParams(vmem_limit_bytes=KERNEL_VMEM),
        name="solve",
    )(flags, table, own, near, far)


def update_kernel(members, rows, cols, blocks, offsets, flags_ref, upper, lower, *rest):
    pieces, out_ref = rest[:len(offsets)], rest[-1]
    plane = pl.program_id(0)
    groups = cols // blocks // LANES
    for b in range(blocks):
        columns = []
        for s in range(b * groups, (b + 1) * groups):
            columns.append(jnp.concatenate([piece[at + plane, s] for piece, at in zip(pieces, offsets)], axis=0))
        x = jnp.concatenate(columns, axis=1) if groups > 1 else columns[0]
        mine = (b + blocks - flags_ref[ME]) % blocks
        total = jnp.dot(upper[mine], x, preferred_element_type=jnp.float32)
        total = total + jnp.dot(lower[mine], x, preferred_element_type=jnp.float32)
        total = total.reshape(members, rows, groups * LANES).astype(jnp.bfloat16)
        out_ref[:, 0, :, b * groups * LANES:(b + 1) * groups * LANES] = total


def update(flags, upper, lower, pieces, offsets, start, count, held, members, planes, rows, cols):
    blocks = upper.shape[0]
    in_specs = [pl.BlockSpec(memory_space=pltpu.SMEM)]
    in_specs += [pl.BlockSpec(memory_space=pltpu.VMEM)] * (2 + len(pieces))
    args = [flags, upper, lower, *(near_core(piece) for piece in pieces)]
    aliases = {}
    if held is not None:
        aliases = {len(args): 0}
        in_specs.append(pl.BlockSpec(memory_space=pl.ANY))
        args.append(held)
    return pl.pallas_call(
        lambda *refs: update_kernel(members, rows, cols, blocks, offsets, *refs),
        grid=(count,),
        in_specs=in_specs,
        out_specs=pl.BlockSpec((members, 1, rows, cols), lambda i: (0, start + i, 0, 0)),
        out_shape=jax.ShapeDtypeStruct((members, planes, rows, cols), jnp.bfloat16),
        input_output_aliases=aliases,
        compiler_params=pltpu.CompilerParams(vmem_limit_bytes=KERNEL_VMEM),
        name="update",
    )(*args)


def near_core(array):
    return pltpu.with_memory_space_constraint(array, pltpu.VMEM)


def from_member(array, shift):
    count = lax.axis_size("member")
    return lax.ppermute(array, "member", [((i + shift) % count, i) for i in range(count)])


def all_members(array):
    return [array] + [from_member(array, shift) for shift in range(1, lax.axis_size("member"))]


def swap_one(array):
    return lax.ppermute(array, "slab", [(i, i ^ 1) for i in range(lax.axis_size("slab"))])


def swap_two(array):
    pairs = [(i, i + 1) for i in range(1, lax.axis_size("slab") - 1, 2)]
    return lax.ppermute(array, "slab", pairs + [(j, i) for i, j in pairs])


def groups_of(planes):
    sizes = [2] * (planes // 2 - 1) + [1, 1] if planes % 2 == 0 else [1] * planes
    return [(sum(sizes[:i]), size) for i, size in enumerate(sizes)]


def cycle(prior_ensemble_fields, params, influence, obs_cell, obs_value, obs_prec, cutoff):
    highest = lax.Precision.HIGHEST
    fine_grain = lax.Precision.HIGH
    members, fields, rows, levels, cols = prior_ensemble_fields.shape
    planes = fields * levels
    tiles = members // TILE
    devices = lax.axis_size("member")
    slabs = lax.axis_size("slab")
    ensemble = members * devices
    me = lax.axis_index("member")
    place = lax.axis_index("slab")
    dims = (fields, rows, levels, cols)
    x2 = prior_ensemble_fields.reshape(members * fields * rows * levels * (cols // LANES), LANES)

    flags = jnp.stack([place % 2, me, place > 0, place < slabs - 1]).astype(jnp.int32)

    *packed, turned = pack(flags, x2, 0, 1, *dims)
    turned = [(turned, 0)]
    if tiles > 1:
        *more, others = pack(flags, x2, 1, tiles - 1, *dims)
        packed += more
        turned += [(others, i) for i in range(tiles - 1)]
    edges = []
    for i in range(tiles):
        edges.append((near_core(swap_one(packed[2 * i])), near_core(swap_two(packed[2 * i + 1]))))

    columns = obs_cell.shape[2]
    npar = params.shape[1]
    own_small = jnp.concatenate(
        [obs_cell[:, 0].astype(jnp.float32), obs_value[:, 0], obs_prec[:, 0]]
        + [jnp.pad(params.T, ((0, -npar % TILE), (0, columns - members)))]
    )
    smalls = all_members(own_small)
    every_param = jnp.concatenate([small[3 * rows:3 * rows + npar, :members].T for small in smalls])
    values = jnp.stack([small[rows:2 * rows] for small in smalls], axis=1)
    precs = jnp.stack([small[2 * rows:3 * rows] for small in smalls], axis=1)

    coef = jnp.dot(params, influence.astype(jnp.float32), precision=highest)

    fine = groups_of(planes)
    forecasts, own_obs = [], None
    for i in range(tiles):
        splits = fine if i == tiles - 1 else [(0, planes)]
        fields_here, local = turned[i]
        *outs, own_obs = stencil(flags, fields_here, *edges[i], coef, smalls, own_obs, i, local, splits, *dims)
        forecasts.append(outs)
    ens_obs = jnp.stack([jnp.roll(array, shift, axis=2) for shift, array in enumerate(all_members(own_obs))])
    sent = []
    for outs in forecasts:
        arrays = []
        for out in outs:
            arrays.append(all_members(out))
        sent.append(arrays)

    ens_obs = ens_obs.transpose(2, 3, 0, 1, 4, 5).reshape(rows, devices, ensemble, LANES).astype(jnp.float32)
    ybar = jnp.mean(ens_obs, axis=2, keepdims=True)
    ypert = ens_obs - ybar
    weighted = precs * (values - ybar[:, :, 0])
    gram = jnp.einsum("rbeo,rbfo->rbef", ypert * precs[:, :, None], ypert, precision=fine_grain)
    gvec = jnp.einsum("rbeo,rbo->rbe", ypert, weighted, precision=highest)
    empty = jnp.zeros((rows, devices, TILE - 1, ensemble), jnp.float32)
    stacked = jnp.concatenate([gram, gvec[:, :, None, :], empty], axis=2)
    stacked = jnp.concatenate([stacked[:, 0::2], stacked[:, 1::2]], axis=3)
    rounded = stacked.astype(jnp.bfloat16)
    near, far = near_core(swap_one(rounded)), near_core(swap_two(rounded))
    radius = cutoff.astype(jnp.float32)
    distance = jnp.abs(jnp.arange(-HALO, HALO + 1, dtype=jnp.float32))[:, None]
    table = jnp.maximum(0.0, 1.0 - distance / (radius + 1.0))
    upper, lower, weight_rows = solve(flags, table, near_core(stacked), near, far, members, ensemble)

    analysis = None
    for g, (start, count) in enumerate(fine):
        pieces, offsets = [], []
        for r in range(devices):
            for arrays in sent:
                pieces.append(arrays[g if len(arrays) > 1 else 0][r])
                offsets.append(0 if len(arrays) > 1 else start)
        analysis = update(flags, upper, lower, pieces, offsets, start, count, analysis, members, planes, rows, cols)
    analysis = analysis.reshape(members, fields, levels, rows, cols).transpose(0, 1, 3, 2, 4)

    pbar = jnp.mean(every_param, axis=0)
    ppert = every_param - pbar
    weight_rows = weight_rows[:, :ensemble] + weight_rows[:, ensemble:]
    part = jnp.einsum("jk,ej->ke", ppert, weight_rows, precision=highest)
    step = 1
    while step < slabs:
        part = part + lax.ppermute(part, "slab", [(i, i ^ step) for i in range(slabs)])
        step *= 2
    total = part / (rows * slabs * devices)
    param_analysis = pbar + total.T
    return (analysis, param_analysis)


def solution(mesh):
    in_specs = (
        P("member", None, "slab", None, None),
        P("member", None),
        P(),
        P("slab", "member", None),
        P("slab", "member", None),
        P("slab", "member", None),
        P("slab"),
    )
    out_specs = (P("member", None, "slab", None, None), P("member", None))
    return jax.shard_map(cycle, mesh=mesh, in_specs=in_specs, out_specs=out_specs, check_vma=False)
```

time: 170 us -> 138 us (0.81)
  the two profiles are of different devices: /device:TPU:10 before, /device:TPU:20 now
where the time goes in v2:
time: 138 us; the launch traced here: 137 us
  Pallas kernels  56.3 us (41%)
  waiting for transfers between devices  49.2 us (36%)
  starting transfers between devices  26.7 us (19%)
  other arithmetic  2.06 us (1%)
  matrix products  1.88 us (1%)
    ppermute x9, waiting for transfers between devices, from_member(): lax.ppermute(array, 'member', [((i + shift) % count, i) for i in range(co...  28.5 us
    pallas_call x4, Pallas kernels, stencil(): pl.pallas_call(lambda *refs: stencil_kernel(fields, rows, levels, cols, b...  24.3 us
    ppermute x5, starting transfers between devices, swap_two(): return lax.ppermute(array, 'slab', pairs + [(j, i) for i, j in pairs])  11.9 us
    pallas_call x2, Pallas kernels, pack(): pl.pallas_call(lambda *refs: pack_kernel(fields, rows, levels, cols, coun...  11.6 us
    ppermute x4, waiting for transfers between devices, cycle(): lax.ppermute(part, 'slab', [(i, i ^ step) for i in range(slabs)])  11.1 us
    pallas_call x1, Pallas kernels, solve(): pl.pallas_call(lambda *refs: solve_kernel(rows, members, ensemble, pairs,...  10.6 us
    pallas_call x4, Pallas kernels, update(): pl.pallas_call(lambda *refs: update_kernel(members, rows, cols, blocks, o...  9.78 us
    ppermute x5, waiting for transfers between devices, swap_two(): return lax.ppermute(array, 'slab', pairs + [(j, i) for i, j in pairs])  9.55 us
  transfers between devices with their start and end apart: 23, of which 8 were waited for; matrix products, arithmetic and copies ran while one was open for 3% of the time, Pallas kernels for 32%

profile of v2, /device:TPU:20, one launch (start us, length us, event | category | flops | bytes accessed | tf_op | source)
XLA Modules:
  0.0 137.4 jit_solution(9066897252137310732)
XLA Ops:
  0.6 0.6 pad_add_fusion.refs_0_
  1.3 4.0 %pack.3 = (bf16[6,4,8,1024]{3,2,1,0:T(8,128)(2,1)}, bf16[6,4,8,1024]{3,2,1,0:T(8,128)(2,1)}, f32[1,6,8,8,1024]{4,3,2,1,0:T(8,128)}) custom-call(s32[4]{0:T(128)} %pad_add_fusion.refs_0_, f32[12288,128]{1,0:T(8,128)} %bitcast.41), custom_call_target="tpu_custom_call" | custom-call | tf_op jit(solution)/shard_map/pack/pallas_call | solution.py:77
  5.3 2.5 %collective-permute-start.8 = (bf16[6,4,8,1024]{3,2,1,0:T(8,128)(2,1)}, bf16[6,4,8,1024]{3,2,1,0:T(8,128)(2,1)S(1)}, u32[]{:S(2)}, u32[]{:S(2)}) collective-permute-start(bf16[6,4,8,1024]{3,2,1,0:T(8,128)(2,1)} %get-tuple-element.35), channel_id=1, source_target_pairs={{1,2},{3,4},{5,6},{7,8},{9,10},{11,12},{13,14},{2,1},{4,3},{6,5},{... | collective-permute-start | bytes 1179656 | tf_op jit(solution)/shard_map/ppermute | solution.py:452
  7.9 1.6 %collective-permute-start.2 = (f32[40,128]{1,0:T(8,128)S(1)}, f32[40,128]{1,0:T(8,128)S(1)}, u32[]{:S(2)}, u32[]{:S(2)}) collective-permute-start(f32[40,128]{1,0:T(8,128)S(1)} %select_maximum_fusion.refs_5_), channel_id=1, source_target_pairs={{16,0},{0,16},{17,1},{1,17},{18,2},{2,18},{19,3},{3,19},{20,4},{4,... | collective-permute-start | bytes 61448 | tf_op jit(solution)/shard_map/ppermute | solution.py:439
  9.5 7.7 %pack.2 = (bf16[6,4,8,1024]{3,2,1,0:T(8,128)(2,1)}, bf16[6,4,8,1024]{3,2,1,0:T(8,128)(2,1)}, bf16[6,4,8,1024]{3,2,1,0:T(8,128)(2,1)}, bf16[6,4,8,1024]{3,2,1,0:T...) custom-call(s32[4]{0:T(128)} %pad_add_fusion.refs_0_, ...), custom_call_target="tpu_custom_call" | custom-call | tf_op jit(solution)/shard_map/pack/pallas_call | solution.py:77
  17.1 0.8 collective-permute-start.5
  18.0 2.7 %collective-permute-start.6 = (bf16[6,4,8,1024]{3,2,1,0:T(8,128)(2,1)}, bf16[6,4,8,1024]{3,2,1,0:T(8,128)(2,1)S(1)}, u32[]{:S(2)}, u32[]{:S(2)}) collective-permute-start(bf16[6,4,8,1024]{3,2,1,0:T(8,128)(2,1)} %get-tuple-element.32), channel_id=1, source_target_pairs={{1,2},{3,4},{5,6},{7,8},{9,10},{11,12},{13,14},{2,1},{4,3},{6,5},{... | collective-permute-start | bytes 1179656 | tf_op jit(solution)/shard_map/ppermute | solution.py:452
  20.7 0.2 fusion.15.refs_4_
  20.9 0.1 reduce_sum.30
  21.1 1.0 collective-permute-start.3
  22.2 1.9 %collective-permute-start.4 = (bf16[6,4,8,1024]{3,2,1,0:T(8,128)(2,1)}, bf16[6,4,8,1024]{3,2,1,0:T(8,128)(2,1)S(1)}, u32[]{:S(2)}, u32[]{:S(2)}) collective-permute-start(bf16[6,4,8,1024]{3,2,1,0:T(8,128)(2,1)} %get-tuple-element.30), channel_id=1, source_target_pairs={{1,2},{3,4},{5,6},{7,8},{9,10},{11,12},{13,14},{2,1},{4,3},{6,5},{... | collective-permute-start | bytes 1179656 | tf_op jit(solution)/shard_map/ppermute | solution.py:452
  24.1 1.0 collective-permute-start
  25.0 2.8 %collective-permute-start.1 = (bf16[6,4,8,1024]{3,2,1,0:T(8,128)(2,1)}, bf16[6,4,8,1024]{3,2,1,0:T(8,128)(2,1)S(1)}, u32[]{:S(2)}, u32[]{:S(2)}) collective-permute-start(bf16[6,4,8,1024]{3,2,1,0:T(8,128)(2,1)} %get-tuple-element.28), channel_id=1, source_target_pairs={{1,2},{3,4},{5,6},{7,8},{9,10},{11,12},{13,14},{2,1},{4,3},{6,5},{... | collective-permute-start | bytes 1179656 | tf_op jit(solution)/shard_map/ppermute | solution.py:452
  28.0 6.1 %stencil.4 = (bf16[6,8,64,128]{3,2,1,0:T(8,128)(2,1)S(1)}, bf16[4,8,2,8,128]{4,3,2,1,0:T(8,128)(2,1)S(1)}) custom-call(s32[4]{0:T(128)S(1)} %copy-done, f32[1,6,8,8,1024]{4,3,2,1,0:T(8,128)} %get-tuple-element.33.refs_1_, bf16[6,4,8,1024]{3,2,1,0:T(8,128)(2,1)S(1)} %collective-permute-done.7.refs_2_, ...), custom_call_target="tpu_custom_call" | custom-call | tf_op jit(solution)/shard_map/stencil/pallas_call | solution.py:240
  34.1 5.8 %collective-permute-done.6.refs_3_ = bf16[6,4,8,1024]{3,2,1,0:T(8,128)(2,1)S(1)} collective-permute-done((bf16[6,4,8,1024]{3,2,1,0:T(8,128)(2,1)}, bf16[6,4,8,1024]{3,2,1,0:T(8,128)(2,1)S(1)}, u32[]{:S(2)}, u32[]{:S(2)}) %collective-permute-start.6) | collective-permute-done | bytes 393248 | tf_op jit(solution)/shard_map/ppermute | solution.py:452
  39.9 6.1 %stencil.5 = (bf16[6,8,64,128]{3,2,1,0:T(8,128)(2,1)S(1)}, bf16[4,8,2,8,128]{4,3,2,1,0:T(8,128)(2,1)S(1)}) custom-call(s32[4]{0:T(128)S(1)} %copy-done, f32[3,6,8,8,1024]{4,3,2,1,0:T(8,128)} %get-tuple-element.26.refs_1_, bf16[6,4,8,1024]{3,2,1,0:T(8,128)(2,1)S(1)} %collective-permute-done.5.refs_2_, ...), custom_call_target="tpu_custom_call", output_to_operand_aliasing={{1}: (7, {})} | custom-call | tf_op jit(solution)/shard_map/stencil/pallas_call | solution.py:240
  46.0 6.1 %stencil.6 = (bf16[6,8,64,128]{3,2,1,0:T(8,128)(2,1)S(1)}, bf16[4,8,2,8,128]{4,3,2,1,0:T(8,128)(2,1)S(1)}) custom-call(s32[4]{0:T(128)S(1)} %copy-done, f32[3,6,8,8,1024]{4,3,2,1,0:T(8,128)} %get-tuple-element.26.refs_1_, bf16[6,4,8,1024]{3,2,1,0:T(8,128)(2,1)S(1)} %collective-permute-done.3.refs_2_, ...), custom_call_target="tpu_custom_call", output_to_operand_aliasing={{1}: (7, {})} | custom-call | tf_op jit(solution)/shard_map/stencil/pallas_call | solution.py:240
  52.1 6.1 %stencil.7 = (bf16[2,8,64,128]{3,2,1,0:T(8,128)(2,1)S(1)}, bf16[2,8,64,128]{3,2,1,0:T(8,128)(2,1)S(1)}, bf16[1,8,64,128]{3,2,1,0:T(8,128)(2,1)S(1)}, bf16[1,8,64...) custom-call(s32[4]{0:T(128)S(1)} %copy-done, ...), custom_call_target="tpu_custom_call", output_to_operand_aliasing={{4}: (7, {})} | custom-call | tf_op jit(solution)/shard_map/stencil/pallas_call | solution.py:240
  58.2 0.6 collective-permute-start.9
  58.8 1.5 %collective-permute-start.14 = (bf16[6,8,64,128]{3,2,1,0:T(8,128)(2,1)S(1)}, bf16[6,8,64,128]{3,2,1,0:T(8,128)(2,1)S(1)}, u32[]{:S(2)}, u32[]{:S(2)}) collective-permute-start(bf16[6,8,64,128]{3,2,1,0:T(8,128)(2,1)S(1)} %get-tuple-element.44.refs_5_), channel_id=1, source_target_pairs={{16,0},{0,16},{17,1},{1,17},{18,2},{2,18},{19,3},{3,19},{20,4},{4,... | collective-permute-start | bytes 2359304 | tf_op jit(solution)/shard_map/ppermute | solution.py:439
  60.3 0.5 collective-permute-start.13
  60.9 1.5 %collective-permute-start.12 = (bf16[6,8,64,128]{3,2,1,0:T(8,128)(2,1)S(1)}, bf16[6,8,64,128]{3,2,1,0:T(8,128)(2,1)S(1)}, u32[]{:S(2)}, u32[]{:S(2)}) collective-permute-start(bf16[6,8,64,128]{3,2,1,0:T(8,128)(2,1)S(1)} %get-tuple-element.42.refs_3_), channel_id=1, source_target_pairs={{16,0},{0,16},{17,1},{1,17},{18,2},{2,18},{19,3},{3,19},{20,4},{4,... | collective-permute-start | bytes 2359304 | tf_op jit(solution)/shard_map/ppermute | solution.py:439
  62.3 2.3 %collective-permute-done.9 = bf16[4,8,2,8,128]{4,3,2,1,0:T(8,128)(2,1)S(1)} collective-permute-done((bf16[4,8,2,8,128]{4,3,2,1,0:T(8,128)(2,1)S(1)}, bf16[4,8,2,8,128]{4,3,2,1,0:T(8,128)(2,1)S(1)}, u32[]{:S(2)}, u32[]{:S(2)}) %collective-permute-start.9) | collective-permute-done | bytes 131104 | tf_op jit(solution)/shard_map/ppermute | solution.py:439
  65.0 0.6 fusion
  65.5 0.9 fusion.12
  66.6 0.1 fusion.18
  66.9 2.1 %collective-permute-start.11 = (bf16[8,1,72,128]{3,2,1,0:T(8,128)(2,1)S(1)}, bf16[8,1,72,128]{3,2,1,0:T(8,128)(2,1)S(1)}, u32[]{:S(2)}, u32[]{:S(2)}) collective-permute-start(bf16[8,1,72,128]{3,2,1,0:T(8,128)(2,1)S(1)} %get-tuple-element.58), channel_id=1, source_target_pairs={{1,2},{3,4},{5,6},{7,8},{9,10},{11,12},{13,14},{2,1},{4,3},{6,5},{... | collective-permute-start | bytes 442376 | tf_op jit(solution)/shard_map/ppermute | solution.py:452
  69.0 0.6 collective-permute-start.18
  69.6 3.7 %collective-permute-done.11.refs_4_ = bf16[8,1,72,128]{3,2,1,0:T(8,128)(2,1)S(1)} collective-permute-done((bf16[8,1,72,128]{3,2,1,0:T(8,128)(2,1)S(1)}, bf16[8,1,72,128]{3,2,1,0:T(8,128)(2,1)S(1)}, u32[]{:S(2)}, u32[]{:S(2)}) %collective-permute-start.11) | collective-permute-done | bytes 147488 | tf_op jit(solution)/shard_map/ppermute | solution.py:452
  73.3 10.6 %solve.1 = (bf16[2,256,512]{2,1,0:T(8,128)(2,1)S(1)}, bf16[2,256,512]{2,1,0:T(8,128)(2,1)S(1)}, f32[32,128]{1,0:T(8,128)S(1)}) custom-call(s32[4]{0:T(128)S(1)} %copy-done, f32[17,8]{1,0:T(8,128)S(1)} %fusion.7.refs_1_, f32[8,1,72,128]{3,2,1,0:T(8,128)S(1)} %get-tuple-element.59.refs_2_, bf16[8,1,72,128]{3,2,1,0:T(8,128)(2,1)S(1)} %collective-permute-done.10.refs_3_, ...), custom_call_target="tpu_custom_call" | custom-call | tf_op jit(solution)/shard_map/solve/pallas_call | solution.py:380
  83.9 0.2 fusion.3
  84.1 1.4 %collective-permute-start.19 = (f32[12,32]{1,0:T(8,128)S(1)}, f32[12,32]{1,0:T(8,128)S(1)}, u32[]{:S(2)}, u32[]{:S(2)}) collective-permute-start(f32[12,32]{1,0:T(8,128)S(1)} %fusion.3), channel_id=1, source_target_pairs={{0,1},{1,0},{2,3},{3,2},{4,5},{5,4},{6,7},{7,6},{8,9},{9,8},{10,11... | collective-permute-start | bytes 4616 | tf_op jit(solution)/shard_map/ppermute | solution.py:546
  85.5 0.8 collective-permute-done.19
  86.3 0.9 collective-permute-start.20
  87.2 2.8 %collective-permute-done.20 = f32[12,32]{1,0:T(8,128)S(1)} collective-permute-done((f32[12,32]{1,0:T(8,128)S(1)}, f32[12,32]{1,0:T(8,128)S(1)}, u32[]{:S(2)}, u32[]{:S(2)}) %collective-permute-start.20) | collective-permute-done | bytes 1568 | tf_op jit(solution)/shard_map/ppermute | solution.py:546
  90.0 0.3 collective-permute-start.21
  90.3 3.3 %collective-permute-done.21 = f32[12,32]{1,0:T(8,128)S(1)} collective-permute-done((f32[12,32]{1,0:T(8,128)S(1)}, f32[12,32]{1,0:T(8,128)S(1)}, u32[]{:S(2)}, u32[]{:S(2)}) %collective-permute-start.21) | collective-permute-done | bytes 1568 | tf_op jit(solution)/shard_map/ppermute | solution.py:546
  93.6 0.5 collective-permute-start.17
  94.2 26.2 %collective-permute-done.18.refs_10_ = bf16[2,8,64,128]{3,2,1,0:T(8,128)(2,1)S(1)} collective-permute-done((bf16[2,8,64,128]{3,2,1,0:T(8,128)(2,1)S(1)}, bf16[2,8,64,128]{3,2,1,0:T(8,128)(2,1)S(1)}, u32[]{:S(2)}, u32[]{:S(2)}) %collective-permute-start.18) | collective-permute-done | bytes 262176 | tf_op jit(solution)/shard_map/ppermute | solution.py:439
  120.3 0.3 collective-permute-start.22
  120.7 4.2 %collective-permute-done.22 = f32[12,32]{1,0:T(8,128)S(1)} collective-permute-done((f32[12,32]{1,0:T(8,128)S(1)}, f32[12,32]{1,0:T(8,128)S(1)}, u32[]{:S(2)}, u32[]{:S(2)}) %collective-permute-start.22) | collective-permute-done | bytes 1568 | tf_op jit(solution)/shard_map/ppermute | solution.py:546
  124.9 0.5 collective-permute-start.16
  125.4 1.5 %collective-permute-start.15 = (bf16[1,8,64,128]{3,2,1,0:T(8,128)(2,1)S(1)}, bf16[1,8,64,128]{3,2,1,0:T(8,128)(2,1)S(1)}, u32[]{:S(2)}, u32[]{:S(2)}) collective-permute-start(bf16[1,8,64,128]{3,2,1,0:T(8,128)(2,1)S(1)} %get-tuple-element.45.refs_6_), channel_id=1, source_target_pairs={{16,0},{0,16},{17,1},{1,17},{18,2},{2,18},{19,3},{3,19},{20,4},{4,... | collective-permute-start | bytes 393224 | tf_op jit(solution)/shard_map/ppermute | solution.py:439
  126.9 0.7 add_bitcast_fusion
  127.6 2.8 %update.4.refs_11_ = bf16[32,6,8,1024]{3,2,1,0:T(8,128)(2,1)} custom-call(s32[4]{0:T(128)S(1)} %copy-done, bf16[2,256,512]{2,1,0:T(8,128)(2,1)S(1)} %get-tuple-element.40.refs_1_, bf16[2,256,512]{2,1,0:T(8,128)(2,1)S(1)} %get-tuple-element.41.refs_2_, bf16[6,8,64,128]{3,2,1,0:T(8,128)(2,1)S(1)} %get-tuple-element.42.refs_3_, ...), custom_call_target="tpu_custom_call" | custom-call | tf_op jit(solution)/shard_map/update/pallas_call | solution.py:421
  130.4 2.8 %update.5.refs_11_ = bf16[32,6,8,1024]{3,2,1,0:T(8,128)(2,1)} custom-call(s32[4]{0:T(128)S(1)} %copy-done, bf16[2,256,512]{2,1,0:T(8,128)(2,1)S(1)} %get-tuple-element.40.refs_1_, bf16[2,256,512]{2,1,0:T(8,128)(2,1)S(1)} %get-tuple-element.41.refs_2_, bf16[6,8,64,128]{3,2,1,0:T(8,128)(2,1)S(1)} %get-tuple-element.42.refs_3_, ...), custom_call_target="tpu_custom_call", output_to_operand_aliasing={{}: (11, {})} | custom-call | tf_op jit(solution)/shard_map/update/pallas_call | solution.py:421
  133.3 2.1 %update.6.refs_11_ = bf16[32,6,8,1024]{3,2,1,0:T(8,128)(2,1)} custom-call(s32[4]{0:T(128)S(1)} %copy-done, bf16[2,256,512]{2,1,0:T(8,128)(2,1)S(1)} %get-tuple-element.40.refs_1_, bf16[2,256,512]{2,1,0:T(8,128)(2,1)S(1)} %get-tuple-element.41.refs_2_, bf16[6,8,64,128]{3,2,1,0:T(8,128)(2,1)S(1)} %get-tuple-element.42.refs_3_, ...), custom_call_target="tpu_custom_call", output_to_operand_aliasing={{}: (11, {})} | custom-call | tf_op jit(solution)/shard_map/update/pallas_call | solution.py:421
  135.3 2.1 %update.7 = bf16[32,6,8,1024]{3,2,1,0:T(8,128)(2,1)} custom-call(s32[4]{0:T(128)S(1)} %copy-done, bf16[2,256,512]{2,1,0:T(8,128)(2,1)S(1)} %get-tuple-element.40.refs_1_, bf16[2,256,512]{2,1,0:T(8,128)(2,1)S(1)} %get-tuple-element.41.refs_2_, bf16[6,8,64,128]{3,2,1,0:T(8,128)(2,1)S(1)} %get-tuple-element.42.refs_3_, ...), custom_call_target="tpu_custom_call", output_to_operand_aliasing={{}: (11, {})} | custom-call | tf_op jit(solution)/shard_map/update/pallas_call | solution.py:421
  (55 shorter events, 1.0 us)
Async XLA Ops:
  1.2 6.6 %copy-start.5 = (s32[8,1,128]{2,1,0:T(1,128)S(1)}, s32[8,1,128]{2,1,0:T(1,128)}, u32[]{:S(2)}) copy-start(s32[8,1,128]{2,1,0:T(1,128)} %param.10) | copy-start | bytes 12292
  1.2 6.6 %copy-start.1 = (f32[32,12]{0,1:T(8,128)S(1)}, f32[32,12]{0,1:T(8,128)}, u32[]{:S(2)}) copy-start(f32[32,12]{0,1:T(8,128)} %param.8) | copy-start | bytes 4612
  1.2 6.6 %copy-start.2 = (f32[8,1,128]{2,1,0:T(1,128)S(1)}, f32[8,1,128]{2,1,0:T(1,128)}, u32[]{:S(2)}) copy-start(f32[8,1,128]{2,1,0:T(1,128)} %param.12) | copy-start | bytes 12292
  1.3 6.6 %copy-start.3 = (f32[8,1,128]{2,1,0:T(1,128)S(1)}, f32[8,1,128]{2,1,0:T(1,128)}, u32[]{:S(2)}) copy-start(f32[8,1,128]{2,1,0:T(1,128)} %param.11) | copy-start | bytes 12292
  5.2 16.9 %collective-permute-start.7 = (bf16[6,4,8,1024]{3,2,1,0:T(8,128)(2,1)}, bf16[6,4,8,1024]{3,2,1,0:T(8,128)(2,1)S(1)}, u32[]{:S(2)}, u32[]{:S(2)}) collective-permute-start(bf16[6,4,8,1024]{3,2,1,0:T(8,128)(2,1)} %get-tuple-element.34), channel_id=1, source_target_pairs={{0,1},{1,0},{2,3},{3,2},{4,5},{5,4},{6,7},{7,6},{8,9},{9,8},{10,11... | collective-permute-start | bytes 1179656 | tf_op jit(solution)/shard_map/ppermute | solution.py:447
  5.3 18.8 %collective-permute-start.8 = (bf16[6,4,8,1024]{3,2,1,0:T(8,128)(2,1)}, bf16[6,4,8,1024]{3,2,1,0:T(8,128)(2,1)S(1)}, u32[]{:S(2)}, u32[]{:S(2)}) collective-permute-start(bf16[6,4,8,1024]{3,2,1,0:T(8,128)(2,1)} %get-tuple-element.35), channel_id=1, source_target_pairs={{1,2},{3,4},{5,6},{7,8},{9,10},{11,12},{13,14},{2,1},{4,3},{6,5},{... | collective-permute-start | bytes 1179656 | tf_op jit(solution)/shard_map/ppermute | solution.py:452
  7.9 12.8 %copy-start.6 = (s32[8]{0:T(128)S(1)}, s32[8]{0:T(128)}, u32[]{:S(2)}) copy-start(s32[8]{0:T(128)} %param.13) | copy-start | bytes 100
  7.9 12.8 %copy-start.4 = (s32[12,6]{0,1:T(8,128)S(1)}, s32[12,6]{0,1:T(8,128)}, u32[]{:S(2)}) copy-start(s32[12,6]{0,1:T(8,128)} %param.9) | copy-start | bytes 868
  7.9 20.1 %copy-start = (s32[4]{0:T(128)S(1)}, s32[4]{0:T(128)}, u32[]{:S(2)}) copy-start(s32[4]{0:T(128)} %pad_add_fusion.refs_0_) | copy-start | bytes 52
  7.9 13.2 %collective-permute-start.2 = (f32[40,128]{1,0:T(8,128)S(1)}, f32[40,128]{1,0:T(8,128)S(1)}, u32[]{:S(2)}, u32[]{:S(2)}) collective-permute-start(f32[40,128]{1,0:T(8,128)S(1)} %select_maximum_fusion.refs_5_), channel_id=1, source_target_pairs={{16,0},{0,16},{17,1},{1,17},{18,2},{2,18},{19,3},{3,19},{20,4},{4,... | collective-permute-start | bytes 61448 | tf_op jit(solution)/shard_map/ppermute | solution.py:439
  17.1 7.9 %collective-permute-start.5 = (bf16[6,4,8,1024]{3,2,1,0:T(8,128)(2,1)}, bf16[6,4,8,1024]{3,2,1,0:T(8,128)(2,1)S(1)}, u32[]{:S(2)}, u32[]{:S(2)}) collective-permute-start(bf16[6,4,8,1024]{3,2,1,0:T(8,128)(2,1)} %get-tuple-element.31), channel_id=1, source_target_pairs={{0,1},{1,0},{2,3},{3,2},{4,5},{5,4},{6,7},{7,6},{8,9},{9,8},{10,11... | collective-permute-start | bytes 1179656 | tf_op jit(solution)/shard_map/ppermute | solution.py:447
  18.0 21.9 %collective-permute-start.6 = (bf16[6,4,8,1024]{3,2,1,0:T(8,128)(2,1)}, bf16[6,4,8,1024]{3,2,1,0:T(8,128)(2,1)S(1)}, u32[]{:S(2)}, u32[]{:S(2)}) collective-permute-start(bf16[6,4,8,1024]{3,2,1,0:T(8,128)(2,1)} %get-tuple-element.32), channel_id=1, source_target_pairs={{1,2},{3,4},{5,6},{7,8},{9,10},{11,12},{13,14},{2,1},{4,3},{6,5},{... | collective-permute-start | bytes 1179656 | tf_op jit(solution)/shard_map/ppermute | solution.py:452
  21.1 24.9 %collective-permute-start.3 = (bf16[6,4,8,1024]{3,2,1,0:T(8,128)(2,1)}, bf16[6,4,8,1024]{3,2,1,0:T(8,128)(2,1)S(1)}, u32[]{:S(2)}, u32[]{:S(2)}) collective-permute-start(bf16[6,4,8,1024]{3,2,1,0:T(8,128)(2,1)} %get-tuple-element.29), channel_id=1, source_target_pairs={{0,1},{1,0},{2,3},{3,2},{4,5},{5,4},{6,7},{7,6},{8,9},{9,8},{10,11... | collective-permute-start | bytes 1179656 | tf_op jit(solution)/shard_map/ppermute | solution.py:447
  22.2 23.9 %collective-permute-start.4 = (bf16[6,4,8,1024]{3,2,1,0:T(8,128)(2,1)}, bf16[6,4,8,1024]{3,2,1,0:T(8,128)(2,1)S(1)}, u32[]{:S(2)}, u32[]{:S(2)}) collective-permute-start(bf16[6,4,8,1024]{3,2,1,0:T(8,128)(2,1)} %get-tuple-element.30), channel_id=1, source_target_pairs={{1,2},{3,4},{5,6},{7,8},{9,10},{11,12},{13,14},{2,1},{4,3},{6,5},{... | collective-permute-start | bytes 1179656 | tf_op jit(solution)/shard_map/ppermute | solution.py:452
  24.1 28.0 %collective-permute-start = (bf16[6,4,8,1024]{3,2,1,0:T(8,128)(2,1)}, bf16[6,4,8,1024]{3,2,1,0:T(8,128)(2,1)S(1)}, u32[]{:S(2)}, u32[]{:S(2)}) collective-permute-start(bf16[6,4,8,1024]{3,2,1,0:T(8,128)(2,1)} %get-tuple-element.27), channel_id=1, source_target_pairs={{0,1},{1,0},{2,3},{3,2},{4,5},{5,4},{6,7},{7,6},{8,9},{9,8},{10,11... | collective-permute-start | bytes 1179656 | tf_op jit(solution)/shard_map/ppermute | solution.py:447
  25.0 27.1 %collective-permute-start.1 = (bf16[6,4,8,1024]{3,2,1,0:T(8,128)(2,1)}, bf16[6,4,8,1024]{3,2,1,0:T(8,128)(2,1)S(1)}, u32[]{:S(2)}, u32[]{:S(2)}) collective-permute-start(bf16[6,4,8,1024]{3,2,1,0:T(8,128)(2,1)} %get-tuple-element.28), channel_id=1, source_target_pairs={{1,2},{3,4},{5,6},{7,8},{9,10},{11,12},{13,14},{2,1},{4,3},{6,5},{... | collective-permute-start | bytes 1179656 | tf_op jit(solution)/shard_map/ppermute | solution.py:452
  58.2 6.4 %collective-permute-start.9 = (bf16[4,8,2,8,128]{4,3,2,1,0:T(8,128)(2,1)S(1)}, bf16[4,8,2,8,128]{4,3,2,1,0:T(8,128)(2,1)S(1)}, u32[]{:S(2)}, u32[]{:S(2)}) collective-permute-start(bf16[4,8,2,8,128]{4,3,2,1,0:T(8,128)(2,1)S(1)} %get-tuple-element.39), channel_id=1, source_target_pairs={{16,0},{0,16},{17,1},{1,17},{18,2},{2,18},{19,3},{3,19},{20,4},{4,... | collective-permute-start | bytes 393224 | tf_op jit(solution)/shard_map/ppermute | solution.py:439
  58.8 66.6 %collective-permute-start.14 = (bf16[6,8,64,128]{3,2,1,0:T(8,128)(2,1)S(1)}, bf16[6,8,64,128]{3,2,1,0:T(8,128)(2,1)S(1)}, u32[]{:S(2)}, u32[]{:S(2)}) collective-permute-start(bf16[6,8,64,128]{3,2,1,0:T(8,128)(2,1)S(1)} %get-tuple-element.44.refs_5_), channel_id=1, source_target_pairs={{16,0},{0,16},{17,1},{1,17},{18,2},{2,18},{19,3},{3,19},{20,4},{4,... | collective-permute-start | bytes 2359304 | tf_op jit(solution)/shard_map/ppermute | solution.py:439
  60.3 67.3 %collective-permute-start.13 = (bf16[6,8,64,128]{3,2,1,0:T(8,128)(2,1)S(1)}, bf16[6,8,64,128]{3,2,1,0:T(8,128)(2,1)S(1)}, u32[]{:S(2)}, u32[]{:S(2)}) collective-permute-start(bf16[6,8,64,128]{3,2,1,0:T(8,128)(2,1)S(1)} %get-tuple-element.43.refs_4_), channel_id=1, source_target_pairs={{16,0},{0,16},{17,1},{1,17},{18,2},{2,18},{19,3},{3,19},{20,4},{4,... | collective-permute-start | bytes 2359304 | tf_op jit(solution)/shard_map/ppermute | solution.py:439
  60.9 66.7 %collective-permute-start.12 = (bf16[6,8,64,128]{3,2,1,0:T(8,128)(2,1)S(1)}, bf16[6,8,64,128]{3,2,1,0:T(8,128)(2,1)S(1)}, u32[]{:S(2)}, u32[]{:S(2)}) collective-permute-start(bf16[6,8,64,128]{3,2,1,0:T(8,128)(2,1)S(1)} %get-tuple-element.42.refs_3_), channel_id=1, source_target_pairs={{16,0},{0,16},{17,1},{1,17},{18,2},{2,18},{19,3},{3,19},{20,4},{4,... | collective-permute-start | bytes 2359304 | tf_op jit(solution)/shard_map/ppermute | solution.py:439
  66.8 2.2 %collective-permute-start.10 = (bf16[8,1,72,128]{3,2,1,0:T(8,128)(2,1)S(1)}, bf16[8,1,72,128]{3,2,1,0:T(8,128)(2,1)S(1)}, u32[]{:S(2)}, u32[]{:S(2)}) collective-permute-start(bf16[8,1,72,128]{3,2,1,0:T(8,128)(2,1)S(1)} %get-tuple-element.58), channel_id=1, source_target_pairs={{0,1},{1,0},{2,3},{3,2},{4,5},{5,4},{6,7},{7,6},{8,9},{9,8},{10,11... | collective-permute-start | bytes 442376 | tf_op jit(solution)/shard_map/ppermute | solution.py:447
  66.9 6.5 %collective-permute-start.11 = (bf16[8,1,72,128]{3,2,1,0:T(8,128)(2,1)S(1)}, bf16[8,1,72,128]{3,2,1,0:T(8,128)(2,1)S(1)}, u32[]{:S(2)}, u32[]{:S(2)}) collective-permute-start(bf16[8,1,72,128]{3,2,1,0:T(8,128)(2,1)S(1)} %get-tuple-element.58), channel_id=1, source_target_pairs={{1,2},{3,4},{5,6},{7,8},{9,10},{11,12},{13,14},{2,1},{4,3},{6,5},{... | collective-permute-start | bytes 442376 | tf_op jit(solution)/shard_map/ppermute | solution.py:452
  69.0 51.3 %collective-permute-start.18 = (bf16[2,8,64,128]{3,2,1,0:T(8,128)(2,1)S(1)}, bf16[2,8,64,128]{3,2,1,0:T(8,128)(2,1)S(1)}, u32[]{:S(2)}, u32[]{:S(2)}) collective-permute-start(bf16[2,8,64,128]{3,2,1,0:T(8,128)(2,1)S(1)} %get-tuple-element.48.refs_6_), channel_id=1, source_target_pairs={{16,0},{0,16},{17,1},{1,17},{18,2},{2,18},{19,3},{3,19},{20,4},{4,... | collective-permute-start | bytes 786440 | tf_op jit(solution)/shard_map/ppermute | solution.py:439
  84.1 2.2 %collective-permute-start.19 = (f32[12,32]{1,0:T(8,128)S(1)}, f32[12,32]{1,0:T(8,128)S(1)}, u32[]{:S(2)}, u32[]{:S(2)}) collective-permute-start(f32[12,32]{1,0:T(8,128)S(1)} %fusion.3), channel_id=1, source_target_pairs={{0,1},{1,0},{2,3},{3,2},{4,5},{5,4},{6,7},{7,6},{8,9},{9,8},{10,11... | collective-permute-start | bytes 4616 | tf_op jit(solution)/shard_map/ppermute | solution.py:546
  86.3 3.7 %collective-permute-start.20 = (f32[12,32]{1,0:T(8,128)S(1)}, f32[12,32]{1,0:T(8,128)S(1)}, u32[]{:S(2)}, u32[]{:S(2)}) collective-permute-start(f32[12,32]{1,0:T(8,128)S(1)} %add.47), channel_id=1, source_target_pairs={{0,2},{1,3},{2,0},{3,1},{4,6},{5,7},{6,4},{7,5},{8,10},{9,11},{10,... | collective-permute-start | bytes 4616 | tf_op jit(solution)/shard_map/ppermute | solution.py:546
  90.0 3.7 %collective-permute-start.21 = (f32[12,32]{1,0:T(8,128)S(1)}, f32[12,32]{1,0:T(8,128)S(1)}, u32[]{:S(2)}, u32[]{:S(2)}) collective-permute-start(f32[12,32]{1,0:T(8,128)S(1)} %add.48), channel_id=1, source_target_pairs={{0,4},{1,5},{2,6},{3,7},{4,0},{5,1},{6,2},{7,3},{8,12},{9,13},{10,... | collective-permute-start | bytes 4616 | tf_op jit(solution)/shard_map/ppermute | solution.py:546
  93.6 36.8 %collective-permute-start.17 = (bf16[2,8,64,128]{3,2,1,0:T(8,128)(2,1)S(1)}, bf16[2,8,64,128]{3,2,1,0:T(8,128)(2,1)S(1)}, u32[]{:S(2)}, u32[]{:S(2)}) collective-permute-start(bf16[2,8,64,128]{3,2,1,0:T(8,128)(2,1)S(1)} %get-tuple-element.47.refs_6_), channel_id=1, source_target_pairs={{16,0},{0,16},{17,1},{1,17},{18,2},{2,18},{19,3},{3,19},{20,4},{4,... | collective-permute-start | bytes 786440 | tf_op jit(solution)/shard_map/ppermute | solution.py:439
  120.3 4.5 %collective-permute-start.22 = (f32[12,32]{1,0:T(8,128)S(1)}, f32[12,32]{1,0:T(8,128)S(1)}, u32[]{:S(2)}, u32[]{:S(2)}) collective-permute-start(f32[12,32]{1,0:T(8,128)S(1)} %add.49), channel_id=1, source_target_pairs={{0,8},{1,9},{2,10},{3,11},{4,12},{5,13},{6,14},{7,15},{8,0},{9,1},... | collective-permute-start | bytes 4616 | tf_op jit(solution)/shard_map/ppermute | solution.py:546
  124.9 8.4 %collective-permute-start.16 = (bf16[1,8,64,128]{3,2,1,0:T(8,128)(2,1)S(1)}, bf16[1,8,64,128]{3,2,1,0:T(8,128)(2,1)S(1)}, u32[]{:S(2)}, u32[]{:S(2)}) collective-permute-start(bf16[1,8,64,128]{3,2,1,0:T(8,128)(2,1)S(1)} %get-tuple-element.46.refs_6_), channel_id=1, source_target_pairs={{16,0},{0,16},{17,1},{1,17},{18,2},{2,18},{19,3},{3,19},{20,4},{4,... | collective-permute-start | bytes 393224 | tf_op jit(solution)/shard_map/ppermute | solution.py:439
  125.4 9.9 %collective-permute-start.15 = (bf16[1,8,64,128]{3,2,1,0:T(8,128)(2,1)S(1)}, bf16[1,8,64,128]{3,2,1,0:T(8,128)(2,1)S(1)}, u32[]{:S(2)}, u32[]{:S(2)}) collective-permute-start(bf16[1,8,64,128]{3,2,1,0:T(8,128)(2,1)S(1)} %get-tuple-element.45.refs_6_), channel_id=1, source_target_pairs={{16,0},{0,16},{17,1},{1,17},{18,2},{2,18},{19,3},{3,19},{20,4},{4,... | collective-permute-start | bytes 393224 | tf_op jit(solution)/shard_map/ppermute | solution.py:439
